TPU v7x, 32 devices: a whole 2x2x4 slice. The times are simulated.
32 devices in a mesh: strip: 2 (over x), swath: 8 (over z, y), group: 2 (over core).
Axes of the slice: x: 2, y: 2, z: 4, core: 2. Of those that a mesh axis runs over, the one named last changes fastest.
Arguments:
- tokens_b: bfloat16 [256, 256, 384], P(('strip', 'swath'), 'group'), parts along dimension 0
- tokens_a: bfloat16 [256, 256, 384], P(('strip', 'swath'), 'group'), parts along dimension 0
- pack_rows: int32 [16, 2, 16, 1024], P(('strip', 'swath'), 'group'), parts along dimension 0, may hold values from 0 to 2047, as said below
- pack_count: int32 [16, 2, 16], P(('strip', 'swath'), 'group'), parts along dimension 0, may hold values from 0 to 1024, as said below
- gather_slots: int32 [4, 256, 256], P(None, ('strip', 'swath'), 'group'), parts along dimension 1, may hold values from 0 to 16383, as said below
- blend_weights: float32 [4, 256, 256], P(None, ('strip', 'swath'), 'group'), parts along dimension 1, may hold values from 0 to 1
- swath_gain: float32 [384], replicated, may hold values from 0.5 to 1.5
- swath_query: bfloat16 [384, 384], replicated
- swath_key: bfloat16 [384, 384], replicated
- swath_value: bfloat16 [384, 384], replicated, may hold values from -0.3125 to 0.3125
- swath_out: bfloat16 [384, 384], replicated, may hold values from -0.3125 to 0.3125
- query_gain: float32 [384], replicated, may hold values from 0.5 to 1.5
- source_gain: float32 [384], replicated, may hold values from 0.5 to 1.5
- cross_query: bfloat16 [384, 384], replicated
- cross_key: bfloat16 [384, 384], replicated
- cross_value: bfloat16 [384, 384], replicated, may hold values from -0.3125 to 0.3125
- cross_out: bfloat16 [384, 384], replicated, may hold values from -0.3125 to 0.3125
- conv_gain: float32 [384], replicated, may hold values from 0.5 to 1.5
- conv_first: bfloat16 [3, 3, 384, 384], replicated, may hold values from -0.109375 to 0.109375
- conv_second: bfloat16 [3, 3, 384, 384], replicated, may hold values from -0.109375 to 0.109375
Outputs:
- merged: bfloat16 [256, 256, 384], P(('strip', 'swath'), 'group'), parts along dimension 0
There are 2 independent parts, one for each index of `strip`. A program takes and returns all parts, laid end to end along the dimension named above; an argument that names none is the same for every part. Nothing has to cross between parts.
Inputs may be any that keep to these rules, and one draw needn't show every extreme that they name: `pack_rows`: entry [s, g, e, c] is a cell of device (s, g)'s block; the first pack_count[s, g, e] entries of a block are distinct. `pack_count`: zero unless the destination device's swath index differs from the source's by at most one; every destination receives exactly 1024 live rows from one of its sources. `gather_slots`: entry [k, i, j] is p * 1024 + c with p a source device whose swath index differs from that of the device holding cell (i, j) by at most one.
All inputs are finite; a program needn't handle non-finite values.
Results may differ from a plain program's by a relative error of at most 0.0095.
Values may be sent and summed in bfloat16 or wider, within the bound.
No kernel may reach another device: no remote copies, remote signals or barrier semaphores. Data moves between devices by JAX's collectives and lax.ppermute only.
A program may use at most 128 MiB of HBM per device.

v0:
```python
import functools

import jax
import jax.numpy as jnp
import numpy as np
from jax import lax
from jax.experimental import pallas as pl
from jax.experimental.pallas import tpu as pltpu
from jax.sharding import PartitionSpec as P


EPSILON = 1e-06
ROWS = 4
SPAN = ROWS + 6
QC = 16
KC = 24
HD = 64

def rms_rows(x, gain):
    inv = lax.rsqrt(jnp.mean(x * x, axis=-1, keepdims=True) + EPSILON)
    return x * inv * gain

def attend_heads(q, k, v, bias):
    rows, lanes = q.shape
    heads = lanes // HD
    lane = lax.broadcasted_iota(jnp.int32, q.shape, 1) // HD
    zero = jnp.zeros_like(q)
    stacked = jnp.concatenate([jnp.where(lane == h, q, zero) for h in range(heads)], axis=0)
    s = lax.dot_general(stacked, k, (((1,), (1,)), ((), ())), preferred_element_type=jnp.float32)
    if bias is not None:
        s = s + jnp.concatenate([bias] * heads, axis=0)
    p = jnp.exp(s - jnp.max(s, axis=-1, keepdims=True))
    total = 1.0 / jnp.sum(p, axis=-1, keepdims=True)
    o = jnp.dot(p.astype(jnp.bfloat16), v, preferred_element_type=jnp.float32)
    mixed, scale = o[:rows], total[:rows]
    for h in range(1, heads):
        mixed = jnp.where(lane == h, o[h * rows:(h + 1) * rows], mixed)
        scale = jnp.where(lane == h, total[h * rows:(h + 1) * rows], scale)
    return mixed * scale

def window_kernel(spans, plan, place_ref, gains_ref, wq_hbm, wk_hbm, wv_hbm, wo_hbm, *rest):
    n_src = len(plan)
    srcs, edges = rest[:n_src], rest[n_src:2 * n_src]
    out_ref, tok, side, normed, qs, kv, mix, wq, wk, wv, wo, sems = rest[2 * n_src:]
    key_rows, breadth, channels = tok.shape
    wide = normed.shape[1]
    rows = ROWS * len(spans)
    copies = []
    for n, (dst0, src0, edge0, count) in enumerate(plan):
        copies.append(pltpu.make_async_copy(edges[n].at[pl.ds(edge0, count)], side.at[pl.ds(dst0, count)], sems.at[4 + 2 * n]))
        copies.append(pltpu.make_async_copy(srcs[n].at[pl.ds(src0, count)], tok.at[pl.ds(dst0, count)], sems.at[5 + 2 * n]))
    weights = [
        pltpu.make_async_copy(src, dst, sems.at[n])
        for n, (src, dst) in enumerate(((wq_hbm, wq), (wk_hbm, wk), (wv_hbm, wv), (wo_hbm, wo)))
    ]
    for c in copies + weights:
        c.start()
    gain = gains_ref[0:1, :]
    normed[:, breadth:, :] = jnp.zeros((key_rows, wide - breadth, channels), jnp.float32)
    n = lax.broadcasted_iota(jnp.int32, (1, SPAN * KC), 1)
    key_row = (n * 2731) >> 16
    key_col = n - key_row * KC
    m = lax.broadcasted_iota(jnp.int32, (ROWS * QC, 1), 0)
    row_gap, col_gap = key_row - (m >> 4), key_col - (m & 15)
    near = (row_gap >= 0) & (row_gap <= 6) & (col_gap >= 0) & (col_gap <= 6)
    row0, col0, height, width = place_ref[0], place_ref[1], place_ref[2], place_ref[3]
    for c in copies:
        c.wait()
    for r in range(key_rows):
        x = rms_rows(tok[r].astype(jnp.float32), gain)
        normed[r, 3:3 + breadth, :] = x
        for n_span, (_, key0) in enumerate(spans):
            if key0 + 3 <= r < key0 + 3 + ROWS:
                qs[n_span * ROWS + r - key0 - 3] = x.astype(jnp.bfloat16)
        x = rms_rows(side[r].astype(jnp.float32), gain)
        normed[r, 0:3, :] = x[5:8]
        normed[r, 3 + breadth:6 + breadth, :] = x[0:3]
    for c in weights:
        c.wait()
    q = jnp.dot(qs[...].reshape(rows * breadth, channels), wq[...], preferred_element_type=jnp.float32)
    qs[...] = (q.astype(jnp.bfloat16) * jnp.bfloat16(HD ** -0.5)).reshape(rows, breadth, channels)
    flat = normed[...].reshape(key_rows * wide, channels).astype(jnp.bfloat16)
    kv[:, :, :channels] = jnp.dot(flat, wk[...], preferred_element_type=jnp.float32).reshape(key_rows, wide, channels)
    kv[:, :, channels:] = jnp.dot(flat, wv[...], preferred_element_type=jnp.float32).reshape(key_rows, wide, channels)

    for n_span, (first_row, key0) in enumerate(spans):
        row_at = key_row + (row0 + first_row - 3)
        inside = jnp.where(near & (row_at >= 0) & (row_at < height), 0.0, -jnp.inf)
        own, keys = slice(n_span * ROWS, n_span * ROWS + ROWS), slice(key0, key0 + SPAN)

        def block(cb, carry):
            c0 = pl.multiple_of(cb * QC, QC)
            col_at = key_col + (col0 + c0 - 3)
            bias = inside + jnp.where((col_at >= 0) & (col_at < width), 0.0, -jnp.inf)
            for l0, l1 in ((0, 256), (256, 384)):
                qp = qs[own, pl.ds(c0, QC), l0:l1].reshape(ROWS * QC, l1 - l0)
                kp = kv[keys, pl.ds(c0, KC), l0:l1].reshape(SPAN * KC, l1 - l0).astype(jnp.bfloat16)
                vp = kv[keys, pl.ds(c0, KC), channels + l0:channels + l1].reshape(SPAN * KC, l1 - l0).astype(jnp.bfloat16)
                mixed = attend_heads(qp, kp, vp, bias)
                mix[own, pl.ds(c0, QC), l0:l1] = mixed.astype(jnp.bfloat16).reshape(ROWS, QC, l1 - l0)
            return carry

        lax.fori_loop(0, breadth // QC, block, 0, unroll=4)
    out = jnp.dot(mix[...].reshape(rows * breadth, channels), wo[...], preferred_element_type=jnp.float32)
    base = jnp.concatenate([tok[key0 + 3:key0 + 3 + ROWS] for _, key0 in spans], axis=0)
    out_ref[...] = (base.astype(jnp.float32).reshape(rows * breadth, channels) + out).astype(jnp.bfloat16)

def window_call(place, gains, wq, wk, wv, wo, spans, parts):
    plan, srcs, edges, at = [], [], [], 0
    for array, edge, first, edge_first, count in parts:
        plan.append((at, first, edge_first, count))
        srcs.append(array)
        edges.append(edge)
        at += count
    breadth, channels = srcs[0].shape[1:]
    wide = breadth + 8
    rows = ROWS * len(spans)
    square = pltpu.VMEM((channels, channels), jnp.bfloat16)
    return pl.pallas_call(
        functools.partial(window_kernel, tuple(spans), tuple(plan)),
        out_shape=jax.ShapeDtypeStruct((rows * breadth, channels), jnp.bfloat16),
        in_specs=[pl.BlockSpec(memory_space=pltpu.SMEM), pl.BlockSpec(memory_space=pltpu.VMEM)]
        + [pl.BlockSpec(memory_space=pltpu.HBM)] * 4 + [pl.BlockSpec(memory_space=pl.ANY)] * (2 * len(srcs)),
        out_specs=pl.BlockSpec(memory_space=pltpu.VMEM),
        scratch_shapes=[
            pltpu.VMEM((at, breadth, channels), jnp.bfloat16),
            pltpu.VMEM((at, 8, channels), jnp.bfloat16),
            pltpu.VMEM((at, wide, channels), jnp.float32),
            pltpu.VMEM((rows, breadth, channels), jnp.bfloat16),
            pltpu.VMEM((at, wide, 2 * channels), jnp.float32),
            pltpu.VMEM((rows, breadth, channels), jnp.bfloat16),
            square, square, square, square,
            pltpu.SemaphoreType.DMA((4 + 2 * len(srcs),)),
        ],
        compiler_params=pltpu.CompilerParams(vmem_limit_bytes=60 << 20),
        cost_estimate=pl.CostEstimate(flops=14_000_000_000, transcendentals=0, bytes_accessed=4_000_000),
    )(place, gains, wq, wk, wv, wo, *srcs, *edges)


TILE = 16
PART = 64
RIM = 2
SIDE = 8
PIECE = 512

def gather_kernel(plan, n_arrays, piece_rows, *refs):
    place_ref, gains_ref, idx_hbm, w_hbm, qa_hbm, ta_hbm, wk_hbm, wv_hbm, wo_hbm = refs[:9]
    arrays = refs[9:9 + n_arrays]
    (joined_ref, normed_ref, top_ref, bottom_ref, edge_ref, table, res, keys, values, mix,
     idx_ref, w_ref, qa_ref, ta_ref, wk_ref, wv_ref, wo_ref, stage, sems, stage_sems) = refs[9 + n_arrays:]
    copies = [
        pltpu.make_async_copy(src, dst, sems.at[n])
        for n, (src, dst) in enumerate((
            (idx_hbm, idx_ref), (w_hbm, w_ref), (wk_hbm, wk_ref), (wv_hbm, wv_ref), (qa_hbm, qa_ref), (ta_hbm, ta_ref), (wo_hbm, wo_ref)))
    ]
    for c in copies:
        c.start()
    height, breadth, channels = ta_ref.shape
    tiles = breadth // TILE
    rows = TILE * TILE
    total = height * breadth
    lanes = channels // 128

    slots = stage.shape[0]

    def copy(n):
        which, first = plan[n]
        return pltpu.make_async_copy(arrays[which].at[pl.ds(first, piece_rows)], stage.at[n % slots], stage_sems.at[n % slots])

    for n in range(slots):
        copy(n).start()
    for n in range(len(plan)):
        copy(n).wait()
        x = stage[n % slots].astype(jnp.float32)
        for j in range(lanes):
            table[pl.ds(n * (piece_rows // 8), piece_rows // 8), j] = x[:, 128 * j:128 * j + 128].reshape(piece_rows // 8, 8, 128)
        if n + slots < len(plan):
            copy(n + slots).start()
    flat = table.reshape(table.shape[0] * lanes * 8, 128)
    out = res.reshape(res.shape[0] * lanes * 8, 128)

    for c in copies[:2]:
        c.wait()

    idx1, w1 = idx_ref.reshape(4 * total), w_ref.reshape(4 * total)

    def line(n, carry):
        row, col = lax.rem(n, TILE), lax.div(n, TILE) * TILE
        at0 = n * (TILE * lanes)
        for j in range(TILE):
            acc = None
            for k in range(4):
                at = k * total + row * breadth + col + j
                term = w1[at] * flat[pl.ds(idx1[at], lanes, stride=8), :]
                acc = term if acc is None else acc + term
            out[pl.ds(at0 + (j // 8) * (8 * lanes) + j % 8, lanes, stride=8), :] = acc
        return carry

    lax.fori_loop(0, tiles * TILE, line, 0)
    for c in copies[2:]:
        c.wait()

    def project(t, carry):
        r = jnp.concatenate([res[pl.ds(t * (rows // 8), rows // 8), j].reshape(rows, 128) for j in range(lanes)], axis=1)
        nr = rms_rows(r.astype(jnp.bfloat16).astype(jnp.float32), gains_ref[2:3, :]).astype(jnp.bfloat16)
        at = pl.ds(pl.multiple_of(t * rows, rows), rows)
        keys[at, :] = jnp.dot(nr, wk_ref[...], preferred_element_type=jnp.float32).astype(jnp.bfloat16)
        values[at, :] = jnp.dot(nr, wv_ref[...], preferred_element_type=jnp.float32).astype(jnp.bfloat16)
        return carry

    lax.fori_loop(0, tiles, project, 0, unroll=2)

    def attend(t, carry):
        at = pl.ds(pl.multiple_of(t * rows, rows), rows)
        qa = qa_ref[:, pl.ds(pl.multiple_of(t * TILE, TILE), TILE), :].reshape(rows, channels)
        for l0, l1 in ((0, 256), (256, 384)):
            kp, vp = keys[at, l0:l1], values[at, l0:l1]
            for q0 in range(0, rows, PART):
                mixed = attend_heads(qa[q0:q0 + PART, l0:l1], kp, vp, None)
                mix[pl.ds(pl.multiple_of(t * rows + q0, PART), PART), l0:l1] = mixed.astype(jnp.bfloat16)
        return carry

    lax.fori_loop(0, tiles, attend, 0, unroll=2)

    def finish(t, carry):
        at = pl.ds(pl.multiple_of(t * rows, rows), rows)
        cols = pl.ds(pl.multiple_of(t * TILE, TILE), TILE)
        o = jnp.dot(mix[at, :], wo_ref[...], preferred_element_type=jnp.float32)
        joined = (ta_ref[:, cols, :].reshape(rows, channels).astype(jnp.float32) + o).astype(jnp.bfloat16)
        joined_ref[:, cols, :] = joined.reshape(TILE, TILE, channels)
        normed_ref[:, cols, :] = rms_rows(joined.astype(jnp.float32), gains_ref[3:4, :]).astype(jnp.bfloat16).reshape(TILE, TILE, channels)
        return carry

    lax.fori_loop(0, tiles, finish, 0, unroll=2)
    top_ref[...] = normed_ref[0:RIM]
    bottom_ref[...] = normed_ref[height - RIM:height]
    first_group = place_ref[1] == 0
    edge_ref[...] = jnp.where(first_group, normed_ref[:, breadth - SIDE:, :], normed_ref[:, 0:SIDE, :])

def gather_call(idx, weights, place, qa, ta, gains, wk, wv, wo, pieces):
    height, breadth, channels = ta.shape
    arrays, plan = [], []
    for rows, first in pieces:
        which = [n for n, array in enumerate(arrays) if array is rows]
        plan.append((which[0] if which else len(arrays), first))
        arrays += [] if which else [rows]
    piece_rows = PIECE
    n = len(pieces)
    total = height * breadth
    lanes = channels // 128
    assert height == TILE and channels == 384
    sm = pl.BlockSpec(memory_space=pltpu.SMEM)
    anywhere = pl.BlockSpec(memory_space=pl.ANY)
    square = pltpu.VMEM((channels, channels), jnp.bfloat16)
    vm = pl.BlockSpec(memory_space=pltpu.VMEM)
    shape = jax.ShapeDtypeStruct((height, breadth, channels), jnp.bfloat16)
    rim = jax.ShapeDtypeStruct((RIM, breadth, channels), jnp.bfloat16)
    return pl.pallas_call(
        functools.partial(gather_kernel, tuple(plan), len(arrays), piece_rows),
        out_shape=(shape, shape, rim, rim, jax.ShapeDtypeStruct((height, SIDE, channels), jnp.bfloat16)),
        in_specs=[sm, vm] + [anywhere] * 3 + [pl.BlockSpec(memory_space=pltpu.HBM)] * 4 + [anywhere] * len(arrays),
        out_specs=(vm,) * 5,
        scratch_shapes=[
            pltpu.VMEM((n * piece_rows // 8, lanes, 8, 128), jnp.float32),
            pltpu.VMEM((total // 8, lanes, 8, 128), jnp.float32),
            pltpu.VMEM((total, channels), jnp.bfloat16),
            pltpu.VMEM((total, channels), jnp.bfloat16),
            pltpu.VMEM((total, channels), jnp.bfloat16),
            pltpu.SMEM(idx.shape, jnp.int32),
            pltpu.SMEM(idx.shape, jnp.float32),
            pltpu.VMEM(ta.shape, jnp.bfloat16),
            pltpu.VMEM(ta.shape, jnp.bfloat16),
            square, square, square,
            pltpu.VMEM((8, piece_rows, channels), jnp.bfloat16),
            pltpu.SemaphoreType.DMA((7,)),
            pltpu.SemaphoreType.DMA((8,)),
        ],
        compiler_params=pltpu.CompilerParams(vmem_limit_bytes=60 << 20),
        cost_estimate=pl.CostEstimate(flops=30_000_000_000, transcendentals=0, bytes_accessed=10_000_000),
    )(place, gains, idx, weights, qa, ta, wk, wv, wo, *arrays)


STEP1, STEP2 = 7, 6

def gelu(x):
    return 0.5 * x * (1.0 + jnp.tanh(0.7978845608028654 * (x + 0.044715 * (x * x * x))))

def tap_copies(src, dst, sems):
    channels = src.shape[-1]
    return [
        pltpu.make_async_copy(
            src.at[a, b], dst.at[pl.ds(a * channels, channels), pl.ds(b * channels, channels)], sems.at[3 * a + b])
        for a in range(3) for b in range(3)
    ]

def conv_rows(src, rows, count, w_ref):
    span, channels = src.shape[1], src.shape[2]
    lhs = [jnp.concatenate([src[pl.ds(row + a, count)] for a in range(3)], axis=-1) for row in rows]
    lhs = lhs[0] if len(lhs) == 1 else jnp.concatenate(lhs, axis=0)
    n = len(rows) * count * span
    y = jnp.dot(lhs.reshape(n, 3 * channels), w_ref[...], preferred_element_type=jnp.float32)
    return (pltpu.roll(y[:, :channels], 1, 0) + y[:, channels:2 * channels]
            + pltpu.roll(y[:, 2 * channels:], n - 1, 0)).reshape(len(rows) * count, span, channels)

def place_sides(field, rows, edge, place_ref, breadth):
    zero = jnp.zeros_like(edge)
    field[rows, 0:SIDE, :] = jnp.where(place_ref[1] > 0, edge, zero)
    field[rows, SIDE + breadth:, :] = jnp.where(place_ref[1] + breadth < place_ref[3], edge, zero)

def columns_inside(place_ref, span):
    col = lax.broadcasted_iota(jnp.int32, (1, span, 1), 1) + (place_ref[1] - SIDE)
    return (col >= 0) & (col < place_ref[3])

def first_kernel(step, place_ref, nc_ref, side_ref, w_hbm, inner_ref, field, w, sems):
    height, breadth, channels = nc_ref.shape
    span = field.shape[1]
    copies = tap_copies(w_hbm, w, sems)
    for c in copies:
        c.start()
    field[:, SIDE:SIDE + breadth, :] = nc_ref[...]
    place_sides(field, slice(0, height), side_ref[...], place_ref, breadth)
    ok = columns_inside(place_ref, span)
    for c in copies:
        c.wait()

    def rows(n, carry):
        x = gelu(conv_rows(field, (n * step,), step, w))
        inner_ref[pl.ds(n * step, step)] = jnp.where(ok, x, 0.0).astype(jnp.bfloat16)
        return carry

    lax.fori_loop(0, (height - 2) // step, rows, 0)

def second_kernel(step, inner_ref, joined_ref, w_hbm, out_ref, w, sems):
    height, breadth, channels = joined_ref.shape
    copies = tap_copies(w_hbm, w, sems)
    for c in copies:
        c.start()
    for c in copies:
        c.wait()

    def rows(n, carry):
        y = conv_rows(inner_ref, (n * step,), step, w)[:, SIDE:SIDE + breadth, :]
        at = pl.ds(n * step + RIM, step)
        out_ref[at] = (joined_ref[at].astype(jnp.float32) + y).astype(jnp.bfloat16)
        return carry

    lax.fori_loop(0, (height - 2 * RIM) // step, rows, 0)

def rim_kernel(place_ref, nc_ref, side_ref, top_ref, bottom_ref, side_rim_ref, inner_ref, joined_ref,
               w1_hbm, w2_hbm, merged_hbm, out_hbm, field, inner, done, w1, w2, sems1, sems2, out_sems):
    height, breadth, channels = joined_ref.shape
    span = field.shape[1]
    copies1, copies2 = tap_copies(w1_hbm, w1, sems1), tap_copies(w2_hbm, w2, sems2)
    for c in copies1 + copies2:
        c.start()
    ok = columns_inside(place_ref, span)
    for c in copies1:
        c.wait()
    for end in range(2):
        own = 0 if end == 0 else height - RIM
        at = 2 * RIM * end
        own_at, far_at = (at + RIM, at) if end == 0 else (at, at + RIM)
        far = top_ref if end == 0 else bottom_ref
        field[own_at:own_at + RIM, SIDE:SIDE + breadth, :] = nc_ref[own:own + RIM]
        place_sides(field, slice(own_at, own_at + RIM), side_ref[own:own + RIM], place_ref, breadth)
        field[far_at:far_at + RIM, SIDE:SIDE + breadth, :] = far[...]
        place_sides(field, slice(far_at, far_at + RIM), side_rim_ref[end * RIM:end * RIM + RIM], place_ref, breadth)
    x = gelu(conv_rows(field, (0, 2 * RIM), RIM, w1))
    n = lax.broadcasted_iota(jnp.int32, (2 * RIM, 1, 1), 0)
    row = place_ref[0] + n + jnp.where(n < RIM, -1, height - 1 - RIM)
    x = jnp.where((row >= 0) & (row < place_ref[2]) & ok, x, 0.0).astype(jnp.bfloat16)
    inner[0:RIM] = x[:RIM]
    inner[RIM:2 * RIM] = inner_ref[0:RIM]
    inner[2 * RIM:3 * RIM] = inner_ref[height - 2 - RIM:height - 2]
    inner[3 * RIM:4 * RIM] = x[RIM:]
    for c in copies2:
        c.wait()
    y = conv_rows(inner, (0, 2 * RIM), RIM, w2)[:, SIDE:SIDE + breadth, :]
    stores = []
    for end in range(2):
        own = 0 if end == 0 else height - RIM
        done[end] = (joined_ref[own:own + RIM].astype(jnp.float32) + y[end * RIM:end * RIM + RIM]).astype(jnp.bfloat16)
        stores.append(pltpu.make_async_copy(done.at[end], out_hbm.at[pl.ds(own, RIM)], out_sems.at[end]))
        stores[end].start()
    for c in stores:
        c.wait()

SM = pl.BlockSpec(memory_space=pltpu.SMEM)
VM = pl.BlockSpec(memory_space=pltpu.VMEM)
HB = pl.BlockSpec(memory_space=pl.ANY)

def first_call(place, nc, side, w1):
    height, breadth, channels = nc.shape
    span = breadth + 2 * SIDE
    return pl.pallas_call(
        functools.partial(first_kernel, STEP1),
        out_shape=jax.ShapeDtypeStruct((height - 2, span, channels), jnp.bfloat16),
        in_specs=[SM, VM, VM, HB],
        out_specs=VM,
        scratch_shapes=[
            pltpu.VMEM((height, span, channels), jnp.bfloat16),
            pltpu.VMEM((3 * channels, 3 * channels), jnp.bfloat16),
            pltpu.SemaphoreType.DMA((9,)),
        ],
        compiler_params=pltpu.CompilerParams(vmem_limit_bytes=40 << 20),
        cost_estimate=pl.CostEstimate(flops=10_000_000_000, transcendentals=0, bytes_accessed=4_000_000),
    )(place, nc, side, w1)

def second_call(inner, joined, w2):
    channels = joined.shape[-1]
    return pl.pallas_call(
        functools.partial(second_kernel, STEP2),
        out_shape=jax.ShapeDtypeStruct(joined.shape, jnp.bfloat16),
        in_specs=[VM, VM, HB],
        out_specs=VM,
        scratch_shapes=[pltpu.VMEM((3 * channels, 3 * channels), jnp.bfloat16), pltpu.SemaphoreType.DMA((9,))],
        compiler_params=pltpu.CompilerParams(vmem_limit_bytes=40 << 20),
        cost_estimate=pl.CostEstimate(flops=8_000_000_000, transcendentals=0, bytes_accessed=4_000_000),
    )(inner, joined, w2)

def rim_call(place, nc, side, top, bottom, side_rim, inner, joined, w1, w2, merged):
    height, breadth, channels = nc.shape
    span = breadth + 2 * SIDE
    return pl.pallas_call(
        rim_kernel,
        out_shape=jax.ShapeDtypeStruct(joined.shape, jnp.bfloat16),
        in_specs=[SM] + [VM] * 7 + [HB] * 3,
        out_specs=HB,
        input_output_aliases={10: 0},
        scratch_shapes=[
            pltpu.VMEM((4 * RIM, span, channels), jnp.bfloat16),
            pltpu.VMEM((4 * RIM, span, channels), jnp.bfloat16),
            pltpu.VMEM((2, RIM, breadth, channels), jnp.bfloat16),
            pltpu.VMEM((3 * channels, 3 * channels), jnp.bfloat16),
            pltpu.VMEM((3 * channels, 3 * channels), jnp.bfloat16),
            pltpu.SemaphoreType.DMA((9,)),
            pltpu.SemaphoreType.DMA((9,)),
            pltpu.SemaphoreType.DMA((2,)),
        ],
        compiler_params=pltpu.CompilerParams(vmem_limit_bytes=40 << 20),
        cost_estimate=pl.CostEstimate(flops=5_000_000_000, transcendentals=0, bytes_accessed=4_000_000),
    )(place, nc, side, top, bottom, side_rim, inner, joined, w1, w2, merged)

def pack_kernel(place_ref, rows_ref, count_ref, keep_ref, give_ref):
    swath, group, groups = place_ref[4], place_ref[5], place_ref[6]
    peers, cap = rows_ref.shape
    lines = cap // 128
    for step in range(3):
        near = jnp.clip(swath + step - 1, 0, peers // groups - 1) * groups
        for ref, at in ((keep_ref, near + group), (give_ref, near + 1 - group)):
            row = rows_ref[pl.ds(at, 1), :]
            for n in range(lines):
                ref[step, n:n + 1, :] = row[:, 128 * n:128 * n + 128]
            ref[step, lines:lines + 1, :] = jnp.full((1, 128), count_ref[0, at], jnp.int32)


def pack_call(place, rows, count):
    sm = pl.BlockSpec(memory_space=pltpu.SMEM)
    vm = pl.BlockSpec(memory_space=pltpu.VMEM)
    shape = jax.ShapeDtypeStruct((3, rows.shape[1] // 128 + 1, 128), jnp.int32)
    return pl.pallas_call(
        pack_kernel, out_shape=(shape, shape), in_specs=[sm, vm, sm], out_specs=(vm, vm),
        cost_estimate=pl.CostEstimate(flops=1_000_000, transcendentals=0, bytes_accessed=100_000),
    )(place, rows, count)


def index_kernel(place_ref, slots_ref, weights_ref, upper_ref, keep_ref, taken_ref, lower_ref, index_ref, live_ref):
    swath, group, groups, cap, block = (place_ref[n] for n in range(4, 9))
    lines = keep_ref.shape[1] - 1
    blocks = ((upper_ref, 0), (upper_ref, 1), (keep_ref, 1), (taken_ref, 1), (lower_ref, 0), (lower_ref, 1))
    slots = slots_ref[...]
    peer, place = lax.div(slots, cap), lax.rem(slots, cap)
    step = lax.div(peer, groups) - swath
    other = jnp.where(lax.rem(peer, groups) == group, 0, 1)
    source = (step + 1) * 2 + other
    line, lane = source * lines + lax.div(place, 128), lax.rem(place, 128)
    cell = jnp.zeros_like(slots)
    count = jnp.zeros_like(slots)
    for s, (ref, at) in enumerate(blocks):
        count = jnp.where(source == s, jnp.broadcast_to(ref[at, lines:lines + 1, :], slots.shape), count)
        for n in range(lines):
            row = jnp.broadcast_to(ref[at, n:n + 1, :], slots.shape)
            picked = jnp.take_along_axis(row, lane, axis=1)
            cell = jnp.where(line == s * lines + n, picked, cell)
    toward = jnp.where(lax.rem(swath, 2) == 0, 1, -1)
    slot = jnp.where(step == 0, 0, jnp.where(step == toward, 1, 2))
    row = (slot * 2 + other) * block + cell
    index_ref[...] = lax.div(row, 8) * (8 * 3) + lax.rem(row, 8)
    live_ref[...] = jnp.where(place < count, weights_ref[...], 0.0)


def index_call(place, slots, weights, tables):
    sm = pl.BlockSpec(memory_space=pltpu.SMEM)
    vm = pl.BlockSpec(memory_space=pltpu.VMEM)
    return pl.pallas_call(
        index_kernel,
        out_shape=(jax.ShapeDtypeStruct(slots.shape, jnp.int32), jax.ShapeDtypeStruct(slots.shape, jnp.float32)),
        in_specs=[sm] + [vm] * 6,
        out_specs=(vm, vm),
        cost_estimate=pl.CostEstimate(flops=1_000_000, transcendentals=0, bytes_accessed=100_000),
    )(place, slots, weights, *tables)


def query_kernel(tokens_ref, gains_ref, w_ref, out_ref):
    height, breadth, channels = tokens_ref.shape
    for r in range(0, height, 4):
        x = rms_rows(tokens_ref[r:r + 4].reshape(4 * breadth, channels).astype(jnp.float32), gains_ref[1:2, :]).astype(jnp.bfloat16)
        q = jnp.dot(x, w_ref[...], preferred_element_type=jnp.float32).astype(jnp.bfloat16)
        out_ref[r:r + 4] = (q * jnp.bfloat16(HD ** -0.5)).reshape(4, breadth, channels)


def query_call(tokens, gains, w):
    return pl.pallas_call(
        query_kernel,
        out_shape=jax.ShapeDtypeStruct(tokens.shape, jnp.bfloat16),
        in_specs=[VM] * 3,
        out_specs=VM,
        compiler_params=pltpu.CompilerParams(vmem_limit_bytes=32 << 20),
        cost_estimate=pl.CostEstimate(flops=1_000_000, transcendentals=0, bytes_accessed=4_000_000),
    )(tokens, gains, w)


def body(
    tokens_b,
    tokens_a,
    pack_rows,
    pack_count,
    gather_slots,
    blend_weights,
    swath_gain,
    swath_query,
    swath_key,
    swath_value,
    swath_out,
    query_gain,
    source_gain,
    cross_query,
    cross_key,
    cross_value,
    cross_out,
    conv_gain,
    conv_first,
    conv_second,
):
    height, breadth, channels = tokens_b.shape
    swaths, groups = lax.axis_size("swath"), lax.axis_size("group")
    swath, group = lax.axis_index("swath"), lax.axis_index("group")
    assert groups == 2 and swaths % 2 == 0
    whole = [height * swaths, breadth * groups]
    down = [(i, i + 1) for i in range(swaths - 1)]
    up = [(j, i) for i, j in down]
    swap = [(0, 1), (1, 0)]
    pairs = [(i, i ^ 1) for i in range(swaths)]
    relay = [(i, j) for i in range(swaths) for j in [i + 2 if i % 2 == 0 else i - 2] if 0 <= j < swaths]

    def inner_edge(field):
        start = (1 - group) * (breadth - SIDE)
        return lax.dynamic_slice_in_dim(field, start, SIDE, axis=1)

    def after(values, *results):
        return lax.optimization_barrier((values, *results))[0]

    cap = pack_rows.shape[-1]
    place = jnp.stack([
        swath * height, group * breadth, jnp.int32(whole[0]), jnp.int32(whole[1]),
        swath, group, jnp.int32(groups), jnp.int32(cap), jnp.int32(height * breadth),
    ]).astype(jnp.int32)
    row = lax.broadcasted_iota(jnp.int32, (8, channels), 0)
    gains = sum(jnp.where(row == n, gain[None, :], 0.0) for n, gain in enumerate((swath_gain, query_gain, source_gain, conv_gain)))

    margin = 3
    side = lax.ppermute(inner_edge(tokens_b), "group", swap)
    top = lax.ppermute(tokens_b[height - margin:], "swath", down)
    bottom = lax.ppermute(tokens_b[:margin], "swath", up)
    projections = (swath_query, swath_key, swath_value, swath_out)

    def near(rows):
        return lax.ppermute(rows, "swath", pairs)

    def far(rows):
        return lax.ppermute(rows, "swath", relay)

    r0, r1, r2, r3 = range(0, height, ROWS)
    middle = window_call(place, gains, *projections, ((r1, 0), (r2, ROWS)), [(tokens_b, side, r1 - margin, r1 - margin, SPAN + ROWS)])
    near_middle = near(middle)
    rims = after(jnp.concatenate([top, bottom], axis=0), middle)
    rims = lax.ppermute(inner_edge(rims), "group", swap)
    ends = window_call(
        after(place, middle), gains, *projections, ((r0, 0), (r3, SPAN)),
        [(top, rims, 0, 0, margin), (tokens_b, side, 0, 0, SPAN - margin),
         (tokens_b, side, r3 - margin, r3 - margin, SPAN - margin), (bottom, rims, 0, margin, margin)],
    )
    near_ends = near(ends)

    pack_rows, pack_count = after((pack_rows, pack_count), near_ends)
    keep, give = pack_call(place, pack_rows.reshape(-1, cap), pack_count.reshape(1, -1))
    taken = lax.ppermute(give, "group", swap)
    upper = lax.ppermute(jnp.concatenate([keep[2:], taken[2:]], axis=0), "swath", down)
    lower = lax.ppermute(jnp.concatenate([keep[:1], taken[:1]], axis=0), "swath", up)
    tokens_a = after(tokens_a, ends)
    index, live = index_call(
        place, gather_slots.reshape(-1, 128), blend_weights.reshape(-1, 128), (upper, keep, taken, lower)
    )
    query_a = query_call(tokens_a, gains, cross_query)

    far_middle = far(near_middle)
    near_ends, query_a = lax.optimization_barrier((near_ends, query_a))
    far_ends = far(near_ends)
    swapped = lambda rows: lax.ppermute(rows, "group", swap)
    blocks = [(middle, ends), (swapped(middle), swapped(ends)), (near_middle, near_ends)]
    blocks += [(swapped(near_middle), swapped(after(near_ends, index, live)))]
    others = (swapped(after(far_middle, index, live)), swapped(far_ends))
    blocks += [(far_middle, far_ends), others]
    size = ROWS * breadth
    pieces = [piece for m, e in blocks for piece in ((e, 0), (m, 0), (m, size), (e, size))]
    joined, normed_c, first_rows, last_rows, edge = gather_call(
        index, live, place, query_a, tokens_a, gains,
        cross_key, cross_value, cross_out, pieces,
    )

    side = lax.ppermute(edge, "group", swap)
    top = lax.ppermute(last_rows, "swath", down)
    bottom = lax.ppermute(first_rows, "swath", up)
    inner = first_call(place, normed_c, side, conv_first)
    rims = after(jnp.concatenate([top, bottom], axis=0), inner)
    rims = lax.ppermute(inner_edge(rims), "group", swap)
    merged = second_call(inner, joined, conv_second)
    return rim_call(place, normed_c, side, top, bottom, rims, inner, joined, conv_first, conv_second, merged)


def solution(mesh):
    rows = P(("strip", "swath"), "group", None)
    maps = P(None, ("strip", "swath"), "group")
    placed = (rows, rows, P(("strip", "swath"), "group", None, None), rows, maps, maps) + (P(),) * 14
    return jax.shard_map(body, mesh=mesh, in_specs=placed, out_specs=rows, check_vma=False)
```

profile of v0, /device:TPU:11, one launch (start us, length us, event | category | flops | bytes accessed | tf_op | source)
XLA Modules:
  0.0 149.2 jit_solution(1748182816729430492)
XLA Ops:
  0.0 0.9 constant_dynamic-slice_fusion.2
  0.9 0.7 collective-permute-start
  1.6 1.1 fusion
  2.8 3.0 %collective-permute-start.2 = (bf16[3,128,384]{2,1,0:T(8,128)(2,1)S(1)}, bf16[3,128,384]{2,1,0:T(8,128)(2,1)S(1)}, u32[]{:S(2)}, u32[]{:S(2)}) collective-permute-start(bf16[3,128,384]{2,1,0:T(8,128)(2,1)S(1)} %get-tuple-element.43), channel_id=1, source_target_pairs={{2,0},{4,2},{6,4},{8,6},{10,8},{12,10},{14,12},{3,1},{5,3},{7,5},{... | collective-permute-start | bytes 884744 | tf_op jit(solution)/shard_map/ppermute | solution.py:574
  5.8 2.2 %collective-permute-start.1 = (bf16[3,128,384]{2,1,0:T(8,128)(2,1)S(1)}, bf16[3,128,384]{2,1,0:T(8,128)(2,1)S(1)}, u32[]{:S(2)}, u32[]{:S(2)}) collective-permute-start(bf16[3,128,384]{2,1,0:T(8,128)(2,1)S(1)} %get-tuple-element.44), channel_id=1, source_target_pairs={{0,2},{2,4},{4,6},{6,8},{8,10},{10,12},{12,14},{1,3},{3,5},{5,7},{... | collective-permute-start | bytes 884744 | tf_op jit(solution)/shard_map/ppermute | solution.py:573
  8.1 1.4 select_add_fusion.gains_ref.refs_1_
  9.5 0.7 stack.19.place_ref.refs_0_
  10.2 0.0 collective-permute-done.rest_1_.rest_5_.rest_6_
  10.2 0.6 copy-done.17
  10.8 13.5 %shard_map.190.refs_10_ = bf16[1024,384]{1,0:T(8,128)(2,1)} custom-call(s32[9]{0:T(128)} %stack.19.place_ref.refs_0_, f32[8,384]{1,0:T(8,128)} %select_add_fusion.gains_ref.refs_1_, bf16[384,384]{1,0:T(8,128)(2,1)} %wq_hbm.3, bf16[384,384]{1,0:T(8,128)(2,1)} %wk_hbm.3, bf16[384,384]{1,0:T(8,128)(2,1)} %wv_hbm.3, bf16[384,384]{1,0:T(8,128)(2,1)} %wo_hbm.3, ...), custom_call_target="tpu_custom_call" | custom-call | flops 14000000000 | bytes 4000000 | tf_op jit(solution)/shard_map/pallas_call | solution.py:119
  24.3 0.0 collective-permute-done.2.rest_3_
  24.3 0.0 collective-permute-done.1.rest_0_
  24.3 0.0 copy-start.11
  24.3 0.1 pad_maximum_fusion
  24.4 0.0 copy-start
  24.5 0.0 copy-start.2
  24.5 0.6 collective-permute-start.3
  25.1 2.2 %collective-permute-start.10 = (bf16[1024,384]{1,0:T(8,128)(2,1)}, bf16[1024,384]{1,0:T(8,128)(2,1)}, u32[]{:S(2)}, u32[]{:S(2)}) collective-permute-start(bf16[1024,384]{1,0:T(8,128)(2,1)} %shard_map.190.refs_10_), channel_id=1, source_target_pairs={{0,2},{2,0},{4,6},{6,4},{8,10},{10,8},{12,14},{14,12},{1,3},{3,1},... | collective-permute-start | bytes 2359304 | tf_op jit(solution)/shard_map/ppermute | solution.py:578
  27.3 0.0 collective-permute-done.3.rest_4_.rest_7_
  27.3 0.6 copy-done.18
  27.9 14.4 %shard_map.191.refs_9_ = bf16[1024,384]{1,0:T(8,128)(2,1)} custom-call(s32[9]{0:T(128)} %stack.19.place_ref.refs_0_, f32[8,384]{1,0:T(8,128)} %select_add_fusion.gains_ref.refs_1_, bf16[384,384]{1,0:T(8,128)(2,1)} %wq_hbm.3, bf16[384,384]{1,0:T(8,128)(2,1)} %wk_hbm.3, bf16[384,384]{1,0:T(8,128)(2,1)} %wv_hbm.3, bf16[384,384]{1,0:T(8,128)(2,1)} %wo_hbm.3, ...), custom_call_target="tpu_custom_call" | custom-call | flops 14000000000 | bytes 4000000 | tf_op jit(solution)/shard_map/pallas_call | solution.py:119
  42.3 0.9 collective-permute-start.4
  43.2 0.6 collective-permute-start.9
  43.8 1.6 %collective-permute-done.10.refs_14_ = bf16[1024,384]{1,0:T(8,128)(2,1)} collective-permute-done((bf16[1024,384]{1,0:T(8,128)(2,1)}, bf16[1024,384]{1,0:T(8,128)(2,1)}, u32[]{:S(2)}, u32[]{:S(2)}) %collective-permute-start.10) | collective-permute-done | bytes 786464 | tf_op jit(solution)/shard_map/ppermute | solution.py:578
  45.4 3.4 %collective-permute-start.14 = (bf16[1024,384]{1,0:T(8,128)(2,1)}, bf16[1024,384]{1,0:T(8,128)(2,1)}, u32[]{:S(2)}, u32[]{:S(2)}) collective-permute-start(bf16[1024,384]{1,0:T(8,128)(2,1)} %collective-permute-done.10.refs_14_), channel_id=1, source_target_pairs={{0,4},{4,8},{6,2},{8,12},{10,6},{14,10},{1,5},{5,9},{7,3},{9,13},{... | collective-permute-start | bytes 2359304 | tf_op jit(solution)/shard_map/ppermute | solution.py:581
  48.9 1.2 shard_map.194.refs_4_
  50.1 0.0 copy-start.1
  50.1 1.1 copy-done.1
  51.2 10.7 %collective-permute-done.4.refs_13_ = bf16[1024,384]{1,0:T(8,128)(2,1)} collective-permute-done((bf16[1024,384]{1,0:T(8,128)(2,1)}, bf16[1024,384]{1,0:T(8,128)(2,1)}, u32[]{:S(2)}, u32[]{:S(2)}) %collective-permute-start.4) | collective-permute-done | bytes 786464 | tf_op jit(solution)/shard_map/ppermute | solution.py:578
  62.0 3.2 %collective-permute-start.13 = (bf16[1024,384]{1,0:T(8,128)(2,1)}, bf16[1024,384]{1,0:T(8,128)(2,1)}, u32[]{:S(2)}, u32[]{:S(2)}) collective-permute-start(bf16[1024,384]{1,0:T(8,128)(2,1)} %collective-permute-done.4.refs_13_), channel_id=1, source_target_pairs={{0,4},{4,8},{6,2},{8,12},{10,6},{14,10},{1,5},{5,9},{7,3},{9,13},{... | collective-permute-start | bytes 2359304 | tf_op jit(solution)/shard_map/ppermute | solution.py:581
  65.2 1.5 %shard_map.192 = (s32[3,9,128]{2,1,0:T(8,128)}, s32[3,9,128]{2,1,0:T(8,128)}) custom-call(s32[9]{0:T(128)} %stack.19.place_ref.refs_0_, s32[16,1024]{1,0:T(8,128)} %bitcast.8, s32[1,16]{1,0:T(1,128)} %bitcast.11), custom_call_target="tpu_custom_call" | custom-call | flops 1000000 | bytes 100000 | tf_op jit(solution)/shard_map/pallas_call | solution.py:461
  66.7 1.2 collective-permute-start.5
  67.9 0.7 fusion.1
  68.6 0.3 collective-permute-done.5.taken_ref
  69.0 2.3 %collective-permute-start.6 = (s32[2,9,128]{2,1,0:T(8,128)S(1)}, s32[2,9,128]{2,1,0:T(8,128)S(1)}, u32[]{:S(2)}, u32[]{:S(2)}) collective-permute-start(s32[2,9,128]{2,1,0:T(8,128)S(1)} %pad_add_fusion), channel_id=1, source_target_pairs={{0,2},{2,4},{4,6},{6,8},{8,10},{10,12},{12,14},{1,3},{3,5},{5,7},{... | collective-permute-start | bytes 27656 | tf_op jit(solution)/shard_map/ppermute | solution.py:598
  71.3 3.9 %collective-permute-start.7 = (s32[2,9,128]{2,1,0:T(8,128)S(1)}, s32[2,9,128]{2,1,0:T(8,128)S(1)}, u32[]{:S(2)}, u32[]{:S(2)}) collective-permute-start(s32[2,9,128]{2,1,0:T(8,128)S(1)} %pad_add_fusion.1), channel_id=1, source_target_pairs={{2,0},{4,2},{6,4},{8,6},{10,8},{12,10},{14,12},{3,1},{5,3},{7,5},{... | collective-permute-start | bytes 27656 | tf_op jit(solution)/shard_map/ppermute | solution.py:599
  75.2 0.0 collective-permute-done.6.upper_ref
  75.2 1.0 collective-permute-start.8
  76.2 0.0 collective-permute-done.7.lower_ref
  76.2 1.3 collective-permute-start.12
  77.5 2.9 %shard_map.193 = (s32[64,128]{1,0:T(8,128)}, f32[64,128]{1,0:T(8,128)}) custom-call(s32[9]{0:T(128)} %stack.19.place_ref.refs_0_, s32[64,128]{1,0:T(8,128)} %bitcast.9, f32[64,128]{1,0:T(8,128)} %bitcast.10, s32[2,9,128]{2,1,0:T(8,128)} %copy-done.13, s32[3,9,128]{2,1,0:T(8,128)} %get-tuple-element.28.keep_ref, s32[3,9,128]{2,1,0:T(8,128)} %copy-done.12, ...), custom_call_target="tpu_custom_call" | custom-call | flops 1000000 | bytes 100000 | tf_op jit(solution)/shard_map/pallas_call | solution.py:495
  80.5 0.0 collective-permute-done.14.refs_18_
  80.5 0.6 collective-permute-start.11
  81.1 0.0 collective-permute-done.9.refs_12_
  81.1 0.1 collective-permute-start.16
  81.2 1.6 %collective-permute-done.13.refs_17_ = bf16[1024,384]{1,0:T(8,128)(2,1)} collective-permute-done((bf16[1024,384]{1,0:T(8,128)(2,1)}, bf16[1024,384]{1,0:T(8,128)(2,1)}, u32[]{:S(2)}, u32[]{:S(2)}) %collective-permute-start.13) | collective-permute-done | bytes 786464 | tf_op jit(solution)/shard_map/ppermute | solution.py:581
  82.9 1.6 %collective-permute-start.15 = (bf16[1024,384]{1,0:T(8,128)(2,1)}, bf16[1024,384]{1,0:T(8,128)(2,1)}, u32[]{:S(2)}, u32[]{:S(2)}) collective-permute-start(bf16[1024,384]{1,0:T(8,128)(2,1)} %collective-permute-done.13.refs_17_), channel_id=1, source_target_pairs={{0,1},{1,0},{2,3},{3,2},{4,5},{5,4},{6,7},{7,6},{8,9},{9,8},{10,11... | collective-permute-start | bytes 2359304 | tf_op jit(solution)/shard_map/ppermute | solution.py:609
  84.4 0.0 collective-permute-done.8.refs_11_
  84.4 0.0 collective-permute-done.12.refs_16_
  84.4 0.0 collective-permute-done.11.refs_15_
  84.4 0.0 collective-permute-done.16.refs_20_
  84.5 2.2 %collective-permute-done.15.refs_19_ = bf16[1024,384]{1,0:T(8,128)(2,1)} collective-permute-done((bf16[1024,384]{1,0:T(8,128)(2,1)}, bf16[1024,384]{1,0:T(8,128)(2,1)}, u32[]{:S(2)}, u32[]{:S(2)}) %collective-permute-start.15) | collective-permute-done | bytes 786464 | tf_op jit(solution)/shard_map/ppermute | solution.py:609
  86.7 29.7 %shard_map.195 = (bf16[16,128,384]{2,1,0:T(8,128)(2,1)}, bf16[16,128,384]{2,1,0:T(8,128)(2,1)}, bf16[2,128,384]{2,1,0:T(8,128)(2,1)}, bf16[2,128,384]{2,1,0:T(8,128)(2,1)}, bf16[16,8,384]{2,1,0:T(8,128)(2,1)}) custom-call(s32[9]{0:T(128)} %stack.19.place_ref.refs_0_, f32[8,384]{1,0:T(8,128)} %select_add_fusion.gains_ref.refs_1_, ...), custom_call_target="tpu_custom_call" | custom-call | flops 30000001024 | bytes 10000000 | tf_op jit(solution)/shard_map/pallas_call | solution.py:258
  116.4 0.4 collective-permute-start.17
  116.9 3.2 %collective-permute-start.18 = (bf16[2,128,384]{2,1,0:T(8,128)(2,1)}, bf16[2,128,384]{2,1,0:T(8,128)(2,1)S(1)}, u32[]{:S(2)}, u32[]{:S(2)}) collective-permute-start(bf16[2,128,384]{2,1,0:T(8,128)(2,1)} %get-tuple-element.39), channel_id=1, source_target_pairs={{0,2},{2,4},{4,6},{6,8},{8,10},{10,12},{12,14},{1,3},{3,5},{5,7},{... | collective-permute-start | bytes 589832 | tf_op jit(solution)/shard_map/ppermute | solution.py:622
  120.1 3.2 %collective-permute-start.19 = (bf16[2,128,384]{2,1,0:T(8,128)(2,1)}, bf16[2,128,384]{2,1,0:T(8,128)(2,1)S(1)}, u32[]{:S(2)}, u32[]{:S(2)}) collective-permute-start(bf16[2,128,384]{2,1,0:T(8,128)(2,1)} %get-tuple-element.40), channel_id=1, source_target_pairs={{2,0},{4,2},{6,4},{8,6},{10,8},{12,10},{14,12},{3,1},{5,3},{7,5},{... | collective-permute-start | bytes 589832 | tf_op jit(solution)/shard_map/ppermute | solution.py:623
  123.3 0.0 collective-permute-done.17.side_ref
  123.3 1.4 copy-done.8
  124.7 9.0 %shard_map.196.inner_ref = bf16[14,144,384]{2,1,0:T(8,128)(2,1)S(1)} custom-call(s32[9]{0:T(128)S(1)} %copy-done.4, bf16[16,128,384]{2,1,0:T(8,128)(2,1)S(1)} %copy-done.8, bf16[16,8,384]{2,1,0:T(8,128)(2,1)S(1)} %collective-permute-done.17.side_ref, bf16[3,3,384,384]{3,2,1,0:T(8,128)(2,1)S(1)} %copy-done.5), custom_call_target="tpu_custom_call" | custom-call | flops 10000000000 | bytes 4000000 | tf_op jit(solution)/shard_map/pallas_call | solution.py:395
  133.8 0.0 collective-permute-done.19.bottom_ref
  133.9 0.8 collective-permute-start.20
  134.7 7.6 %shard_map.197.merged_hbm = bf16[16,128,384]{2,1,0:T(8,128)(2,1)} custom-call(bf16[14,144,384]{2,1,0:T(8,128)(2,1)S(1)} %shard_map.196.inner_ref, bf16[16,128,384]{2,1,0:T(8,128)(2,1)S(1)} %copy-done.7, bf16[3,3,384,384]{3,2,1,0:T(8,128)(2,1)S(1)} %copy-done.6), custom_call_target="tpu_custom_call" | custom-call | flops 8000000000 | bytes 4000000 | tf_op jit(solution)/shard_map/pallas_call | solution.py:411
  142.2 0.0 collective-permute-done.20.side_rim_ref
  142.3 6.8 %shard_map.198 = bf16[16,128,384]{2,1,0:T(8,128)(2,1)} custom-call(s32[9]{0:T(128)S(1)} %copy-done.4, bf16[16,128,384]{2,1,0:T(8,128)(2,1)S(1)} %copy-done.9, bf16[16,8,384]{2,1,0:T(8,128)(2,1)S(1)} %collective-permute-done.17.side_ref, bf16[2,128,384]{2,1,0:T(8,128)(2,1)S(1)} %collective-permute-done.18.top_ref, ...), custom_call_target="tpu_custom_call", output_to_operand_aliasing={{}: (10, {})} | custom-call | flops 5000000000 | bytes 4000000 | tf_op jit(solution)/shard_map/pallas_call | solution.py:424
  (39 shorter events, 0.2 us)
Async XLA Ops:
  0.9 9.3 %collective-permute-start = (bf16[16,8,384]{2,1,0:T(8,128)(2,1)S(1)}, bf16[16,8,384]{2,1,0:T(8,128)(2,1)S(1)}, u32[]{:S(2)}, u32[]{:S(2)}) collective-permute-start(bf16[16,8,384]{2,1,0:T(8,128)(2,1)S(1)} %constant_dynamic-slice_fusion.2), channel_id=1, source_target_pairs={{0,1},{1,0},{2,3},{3,2},{4,5},{5,4},{6,7},{7,6},{8,9},{9,8},{10,11... | collective-permute-start | bytes 294920 | tf_op jit(solution)/shard_map/ppermute | solution.py:572
  2.8 21.5 %collective-permute-start.2 = (bf16[3,128,384]{2,1,0:T(8,128)(2,1)S(1)}, bf16[3,128,384]{2,1,0:T(8,128)(2,1)S(1)}, u32[]{:S(2)}, u32[]{:S(2)}) collective-permute-start(bf16[3,128,384]{2,1,0:T(8,128)(2,1)S(1)} %get-tuple-element.43), channel_id=1, source_target_pairs={{2,0},{4,2},{6,4},{8,6},{10,8},{12,10},{14,12},{3,1},{5,3},{7,5},{... | collective-permute-start | bytes 884744 | tf_op jit(solution)/shard_map/ppermute | solution.py:574
  5.8 18.5 %collective-permute-start.1 = (bf16[3,128,384]{2,1,0:T(8,128)(2,1)S(1)}, bf16[3,128,384]{2,1,0:T(8,128)(2,1)S(1)}, u32[]{:S(2)}, u32[]{:S(2)}) collective-permute-start(bf16[3,128,384]{2,1,0:T(8,128)(2,1)S(1)} %get-tuple-element.44), channel_id=1, source_target_pairs={{0,2},{2,4},{4,6},{6,8},{8,10},{10,12},{12,14},{1,3},{3,5},{5,7},{... | collective-permute-start | bytes 884744 | tf_op jit(solution)/shard_map/ppermute | solution.py:573
  10.2 0.6 copy-start.17
  24.3 3.0 %copy-start.10 = (bf16[3,128,384]{2,1,0:T(8,128)(2,1)}, bf16[3,128,384]{2,1,0:T(8,128)(2,1)S(1)}, u32[]{:S(2)}) copy-start(bf16[3,128,384]{2,1,0:T(8,128)(2,1)S(1)} %collective-permute-done.2.rest_3_) | copy-start | bytes 884740
  24.3 3.0 %copy-start.11 = (bf16[3,128,384]{2,1,0:T(8,128)(2,1)}, bf16[3,128,384]{2,1,0:T(8,128)(2,1)S(1)}, u32[]{:S(2)}) copy-start(bf16[3,128,384]{2,1,0:T(8,128)(2,1)S(1)} %collective-permute-done.1.rest_0_) | copy-start | bytes 884740
  24.4 18.8 %copy-start.15 = (bf16[1024,384]{1,0:T(8,128)(2,1)S(1)}, bf16[1024,384]{1,0:T(8,128)(2,1)}, u32[]{:S(2)}) copy-start(bf16[1024,384]{1,0:T(8,128)(2,1)} %shard_map.190.refs_10_) | copy-start | bytes 2359300
  24.4 24.4 %copy-start = (bf16[16,128,384]{2,1,0:T(8,128)(2,1)S(1)}, bf16[16,128,384]{2,1,0:T(8,128)(2,1)}, u32[]{:S(2)}) copy-start(bf16[16,128,384]{2,1,0:T(8,128)(2,1)} %refs_5_) | copy-start | bytes 4718596
  24.5 24.4 %copy-start.2 = (bf16[384,384]{1,0:T(8,128)(2,1)S(1)}, bf16[384,384]{1,0:T(8,128)(2,1)}, u32[]{:S(2)}) copy-start(bf16[384,384]{1,0:T(8,128)(2,1)} %w_ref.1) | copy-start | bytes 884740
  24.5 24.4 %copy-start.3 = (f32[8,384]{1,0:T(8,128)S(1)}, f32[8,384]{1,0:T(8,128)}, u32[]{:S(2)}) copy-start(f32[8,384]{1,0:T(8,128)} %select_add_fusion.gains_ref.refs_1_) | copy-start | bytes 36868
  24.5 2.8 %collective-permute-start.3 = (bf16[6,8,384]{2,1,0:T(8,128)(2,1)S(1)}, bf16[6,8,384]{2,1,0:T(8,128)(2,1)S(1)}, u32[]{:S(2)}, u32[]{:S(2)}) collective-permute-start(bf16[6,8,384]{2,1,0:T(8,128)(2,1)S(1)} %constant_dynamic-slice_fusion.1), channel_id=1, source_target_pairs={{0,1},{1,0},{2,3},{3,2},{4,5},{5,4},{6,7},{7,6},{8,9},{9,8},{10,11... | collective-permute-start | bytes 110600 | tf_op jit(solution)/shard_map/ppermute | solution.py:587
  25.1 20.3 %collective-permute-start.10 = (bf16[1024,384]{1,0:T(8,128)(2,1)}, bf16[1024,384]{1,0:T(8,128)(2,1)}, u32[]{:S(2)}, u32[]{:S(2)}) collective-permute-start(bf16[1024,384]{1,0:T(8,128)(2,1)} %shard_map.190.refs_10_), channel_id=1, source_target_pairs={{0,2},{2,0},{4,6},{6,4},{8,10},{10,8},{12,14},{14,12},{1,3},{3,1},... | collective-permute-start | bytes 2359304 | tf_op jit(solution)/shard_map/ppermute | solution.py:578
  27.3 0.6 copy-start.18
  42.3 19.7 %collective-permute-start.4 = (bf16[1024,384]{1,0:T(8,128)(2,1)}, bf16[1024,384]{1,0:T(8,128)(2,1)}, u32[]{:S(2)}, u32[]{:S(2)}) collective-permute-start(bf16[1024,384]{1,0:T(8,128)(2,1)} %shard_map.191.refs_9_), channel_id=1, source_target_pairs={{0,2},{2,0},{4,6},{6,4},{8,10},{10,8},{12,14},{14,12},{1,3},{3,1},... | collective-permute-start | bytes 2359304 | tf_op jit(solution)/shard_map/ppermute | solution.py:578
  43.2 37.9 %collective-permute-start.9 = (bf16[1024,384]{1,0:T(8,128)(2,1)S(1)}, bf16[1024,384]{1,0:T(8,128)(2,1)}, u32[]{:S(2)}, u32[]{:S(2)}) collective-permute-start(bf16[1024,384]{1,0:T(8,128)(2,1)S(1)} %copy-done.15), channel_id=1, source_target_pairs={{0,1},{1,0},{2,3},{3,2},{4,5},{5,4},{6,7},{7,6},{8,9},{9,8},{10,11... | collective-permute-start | bytes 2359304 | tf_op jit(solution)/shard_map/ppermute | solution.py:609
  45.4 35.1 %collective-permute-start.14 = (bf16[1024,384]{1,0:T(8,128)(2,1)}, bf16[1024,384]{1,0:T(8,128)(2,1)}, u32[]{:S(2)}, u32[]{:S(2)}) collective-permute-start(bf16[1024,384]{1,0:T(8,128)(2,1)} %collective-permute-done.10.refs_14_), channel_id=1, source_target_pairs={{0,4},{4,8},{6,2},{8,12},{10,6},{14,10},{1,5},{5,9},{7,3},{9,13},{... | collective-permute-start | bytes 2359304 | tf_op jit(solution)/shard_map/ppermute | solution.py:581
  50.1 1.1 copy-start.1
  62.0 20.9 %collective-permute-start.13 = (bf16[1024,384]{1,0:T(8,128)(2,1)}, bf16[1024,384]{1,0:T(8,128)(2,1)}, u32[]{:S(2)}, u32[]{:S(2)}) collective-permute-start(bf16[1024,384]{1,0:T(8,128)(2,1)} %collective-permute-done.4.refs_13_), channel_id=1, source_target_pairs={{0,4},{4,8},{6,2},{8,12},{10,6},{14,10},{1,5},{5,9},{7,3},{9,13},{... | collective-permute-start | bytes 2359304 | tf_op jit(solution)/shard_map/ppermute | solution.py:581
  66.7 2.3 %collective-permute-start.5 = (s32[3,9,128]{2,1,0:T(8,128)}, s32[3,9,128]{2,1,0:T(8,128)S(1)}, u32[]{:S(2)}, u32[]{:S(2)}) collective-permute-start(s32[3,9,128]{2,1,0:T(8,128)} %get-tuple-element.29), channel_id=1, source_target_pairs={{0,1},{1,0},{2,3},{3,2},{4,5},{5,4},{6,7},{7,6},{8,9},{9,8},{10,11... | collective-permute-start | bytes 41480 | tf_op jit(solution)/shard_map/ppermute | solution.py:597
  69.0 8.6 %copy-start.12 = (s32[3,9,128]{2,1,0:T(8,128)}, s32[3,9,128]{2,1,0:T(8,128)S(1)}, u32[]{:S(2)}) copy-start(s32[3,9,128]{2,1,0:T(8,128)S(1)} %collective-permute-done.5.taken_ref) | copy-start | bytes 41476
  69.0 6.2 %collective-permute-start.6 = (s32[2,9,128]{2,1,0:T(8,128)S(1)}, s32[2,9,128]{2,1,0:T(8,128)S(1)}, u32[]{:S(2)}, u32[]{:S(2)}) collective-permute-start(s32[2,9,128]{2,1,0:T(8,128)S(1)} %pad_add_fusion), channel_id=1, source_target_pairs={{0,2},{2,4},{4,6},{6,8},{8,10},{10,12},{12,14},{1,3},{3,5},{5,7},{... | collective-permute-start | bytes 27656 | tf_op jit(solution)/shard_map/ppermute | solution.py:598
  71.3 4.9 %collective-permute-start.7 = (s32[2,9,128]{2,1,0:T(8,128)S(1)}, s32[2,9,128]{2,1,0:T(8,128)S(1)}, u32[]{:S(2)}, u32[]{:S(2)}) collective-permute-start(s32[2,9,128]{2,1,0:T(8,128)S(1)} %pad_add_fusion.1), channel_id=1, source_target_pairs={{2,0},{4,2},{6,4},{8,6},{10,8},{12,10},{14,12},{3,1},{5,3},{7,5},{... | collective-permute-start | bytes 27656 | tf_op jit(solution)/shard_map/ppermute | solution.py:599
  75.2 2.3 %copy-start.13 = (s32[2,9,128]{2,1,0:T(8,128)}, s32[2,9,128]{2,1,0:T(8,128)S(1)}, u32[]{:S(2)}) copy-start(s32[2,9,128]{2,1,0:T(8,128)S(1)} %collective-permute-done.6.upper_ref) | copy-start | bytes 27652
  75.2 9.2 %collective-permute-start.8 = (bf16[1024,384]{1,0:T(8,128)(2,1)}, bf16[1024,384]{1,0:T(8,128)(2,1)}, u32[]{:S(2)}, u32[]{:S(2)}) collective-permute-start(bf16[1024,384]{1,0:T(8,128)(2,1)} %shard_map.191.refs_9_), channel_id=1, source_target_pairs={{0,1},{1,0},{2,3},{3,2},{4,5},{5,4},{6,7},{7,6},{8,9},{9,8},{10,11... | collective-permute-start | bytes 2359304 | tf_op jit(solution)/shard_map/ppermute | solution.py:609
  76.2 1.3 copy-start.14
  76.2 8.2 %collective-permute-start.12 = (bf16[1024,384]{1,0:T(8,128)(2,1)}, bf16[1024,384]{1,0:T(8,128)(2,1)}, u32[]{:S(2)}, u32[]{:S(2)}) collective-permute-start(bf16[1024,384]{1,0:T(8,128)(2,1)} %collective-permute-done.10.refs_14_), channel_id=1, source_target_pairs={{0,1},{1,0},{2,3},{3,2},{4,5},{5,4},{6,7},{7,6},{8,9},{9,8},{10,11... | collective-permute-start | bytes 2359304 | tf_op jit(solution)/shard_map/ppermute | solution.py:609
  80.5 42.8 %copy-start.4 = (s32[9]{0:T(128)S(1)}, s32[9]{0:T(128)}, u32[]{:S(2)}) copy-start(s32[9]{0:T(128)} %stack.19.place_ref.refs_0_) | copy-start | bytes 112
  80.5 42.9 %copy-start.5 = (bf16[3,3,384,384]{3,2,1,0:T(8,128)(2,1)S(1)}, bf16[3,3,384,384]{3,2,1,0:T(8,128)(2,1)}, u32[]{:S(2)}) copy-start(bf16[3,3,384,384]{3,2,1,0:T(8,128)(2,1)} %w1_hbm.1) | copy-start | bytes 7962628
  80.5 4.0 %collective-permute-start.11 = (bf16[1024,384]{1,0:T(8,128)(2,1)}, bf16[1024,384]{1,0:T(8,128)(2,1)}, u32[]{:S(2)}, u32[]{:S(2)}) collective-permute-start(bf16[1024,384]{1,0:T(8,128)(2,1)} %collective-permute-done.4.refs_13_), channel_id=1, source_target_pairs={{0,1},{1,0},{2,3},{3,2},{4,5},{5,4},{6,7},{7,6},{8,9},{9,8},{10,11... | collective-permute-start | bytes 2359304 | tf_op jit(solution)/shard_map/ppermute | solution.py:609
  81.1 3.3 %collective-permute-start.16 = (bf16[1024,384]{1,0:T(8,128)(2,1)}, bf16[1024,384]{1,0:T(8,128)(2,1)S(1)}, u32[]{:S(2)}, u32[]{:S(2)}) collective-permute-start(bf16[1024,384]{1,0:T(8,128)(2,1)} %collective-permute-done.14.refs_18_), channel_id=1, source_target_pairs={{0,1},{1,0},{2,3},{3,2},{4,5},{5,4},{6,7},{7,6},{8,9},{9,8},{10,11... | collective-permute-start | bytes 2359304 | tf_op jit(solution)/shard_map/ppermute | solution.py:609
  82.9 3.8 %collective-permute-start.15 = (bf16[1024,384]{1,0:T(8,128)(2,1)}, bf16[1024,384]{1,0:T(8,128)(2,1)}, u32[]{:S(2)}, u32[]{:S(2)}) collective-permute-start(bf16[1024,384]{1,0:T(8,128)(2,1)} %collective-permute-done.13.refs_17_), channel_id=1, source_target_pairs={{0,1},{1,0},{2,3},{3,2},{4,5},{5,4},{6,7},{7,6},{8,9},{9,8},{10,11... | collective-permute-start | bytes 2359304 | tf_op jit(solution)/shard_map/ppermute | solution.py:609
  84.5 2.2 %copy-start.16 = (bf16[1024,384]{1,0:T(8,128)(2,1)}, bf16[1024,384]{1,0:T(8,128)(2,1)S(1)}, u32[]{:S(2)}) copy-start(bf16[1024,384]{1,0:T(8,128)(2,1)S(1)} %collective-permute-done.16.refs_20_) | copy-start | bytes 2359300
  116.4 6.9 %collective-permute-start.17 = (bf16[16,8,384]{2,1,0:T(8,128)(2,1)}, bf16[16,8,384]{2,1,0:T(8,128)(2,1)S(1)}, u32[]{:S(2)}, u32[]{:S(2)}) collective-permute-start(bf16[16,8,384]{2,1,0:T(8,128)(2,1)} %get-tuple-element.38), channel_id=1, source_target_pairs={{0,1},{1,0},{2,3},{3,2},{4,5},{5,4},{6,7},{7,6},{8,9},{9,8},{10,11... | collective-permute-start | bytes 294920 | tf_op jit(solution)/shard_map/ppermute | solution.py:621
  116.9 16.9 %collective-permute-start.18 = (bf16[2,128,384]{2,1,0:T(8,128)(2,1)}, bf16[2,128,384]{2,1,0:T(8,128)(2,1)S(1)}, u32[]{:S(2)}, u32[]{:S(2)}) collective-permute-start(bf16[2,128,384]{2,1,0:T(8,128)(2,1)} %get-tuple-element.39), channel_id=1, source_target_pairs={{0,2},{2,4},{4,6},{6,8},{8,10},{10,12},{12,14},{1,3},{3,5},{5,7},{... | collective-permute-start | bytes 589832 | tf_op jit(solution)/shard_map/ppermute | solution.py:622
  120.1 13.7 %collective-permute-start.19 = (bf16[2,128,384]{2,1,0:T(8,128)(2,1)}, bf16[2,128,384]{2,1,0:T(8,128)(2,1)S(1)}, u32[]{:S(2)}, u32[]{:S(2)}) collective-permute-start(bf16[2,128,384]{2,1,0:T(8,128)(2,1)} %get-tuple-element.40), channel_id=1, source_target_pairs={{2,0},{4,2},{6,4},{8,6},{10,8},{12,10},{14,12},{3,1},{5,3},{7,5},{... | collective-permute-start | bytes 589832 | tf_op jit(solution)/shard_map/ppermute | solution.py:623
  123.3 1.4 copy-start.8
  124.7 9.9 %copy-start.6 = (bf16[3,3,384,384]{3,2,1,0:T(8,128)(2,1)S(1)}, bf16[3,3,384,384]{3,2,1,0:T(8,128)(2,1)}, u32[]{:S(2)}) copy-start(bf16[3,3,384,384]{3,2,1,0:T(8,128)(2,1)} %w2_hbm.1) | copy-start | bytes 7962628
  124.7 9.9 %copy-start.7 = (bf16[16,128,384]{2,1,0:T(8,128)(2,1)S(1)}, bf16[16,128,384]{2,1,0:T(8,128)(2,1)}, u32[]{:S(2)}) copy-start(bf16[16,128,384]{2,1,0:T(8,128)(2,1)} %get-tuple-element.42.joined_ref) | copy-start | bytes 4718596
  133.9 8.4 %collective-permute-start.20 = (bf16[4,8,384]{2,1,0:T(8,128)(2,1)S(1)}, bf16[4,8,384]{2,1,0:T(8,128)(2,1)S(1)}, u32[]{:S(2)}, u32[]{:S(2)}) collective-permute-start(bf16[4,8,384]{2,1,0:T(8,128)(2,1)S(1)} %constant_dynamic-slice_fusion), channel_id=1, source_target_pairs={{0,1},{1,0},{2,3},{3,2},{4,5},{5,4},{6,7},{7,6},{8,9},{9,8},{10,11... | collective-permute-start | bytes 73736 | tf_op jit(solution)/shard_map/ppermute | solution.py:626
  134.7 7.6 %copy-start.9 = (bf16[16,128,384]{2,1,0:T(8,128)(2,1)S(1)}, bf16[16,128,384]{2,1,0:T(8,128)(2,1)}, u32[]{:S(2)}) copy-start(bf16[16,128,384]{2,1,0:T(8,128)(2,1)} %get-tuple-element.37.nc_ref) | copy-start | bytes 4718596
where the time goes:
time: 150 us; the launch traced here: 149 us
  Pallas kernels  86.6 us (58%)
  starting transfers between devices  36.7 us (24%)
  waiting for transfers between devices  16.5 us (11%)
  local copies, waits for them, and re-layouts  7.26 us (5%)
  other arithmetic  1.55 us (1%)
    pallas_call x1, Pallas kernels, gather_call(): pl.pallas_call(functools.partial(gather_kernel, tuple(plan), len(arrays),...  29.7 us
    pallas_call x2, Pallas kernels, window_call(): pl.pallas_call(functools.partial(window_kernel, tuple(spans), tuple(plan)...  27.9 us
    ppermute x2, waiting for transfers between devices, near(): return lax.ppermute(rows, 'swath', pairs)  12.3 us
    pallas_call x1, Pallas kernels, first_call(): pl.pallas_call(functools.partial(first_kernel, STEP1), out_shape=jax.Shap...  9.03 us
    pallas_call x1, Pallas kernels, second_call(): pl.pallas_call(functools.partial(second_kernel, STEP2), out_shape=jax.Sha...  7.56 us
    pallas_call x1, Pallas kernels, rim_call(): pl.pallas_call(rim_kernel, out_shape=jax.ShapeDtypeStruct(joined.shape, j...  6.76 us
    ppermute x2, starting transfers between devices, far(): return lax.ppermute(rows, 'swath', relay)  6.61 us
    ppermute x6, starting transfers between devices, body(): swapped = lambda rows: lax.ppermute(rows, 'group', swap)  5.25 us
  transfers between devices with their start and end apart: 21, of which 5 were waited for; matrix products, arithmetic and copies ran while one was open for 3% of the time, Pallas kernels for 34%

commit v1 on v0

--- a/solution.py
+++ b/solution.py
@@ -38,10 +38,11 @@
         scale = jnp.where(lane == h, total[h * rows:(h + 1) * rows], scale)
     return mixed * scale
 
-def window_kernel(spans, plan, place_ref, gains_ref, wq_hbm, wk_hbm, wv_hbm, wo_hbm, *rest):
+def window_kernel(spans, plan, place_ref, gain_ref, wq_hbm, wk_hbm, wv_hbm, wo_hbm, *rest):
+    assert len(spans) == 2 and spans[0][1] == 0
     n_src = len(plan)
     srcs, edges = rest[:n_src], rest[n_src:2 * n_src]
-    out_ref, tok, side, normed, qs, kv, mix, wq, wk, wv, wo, sems = rest[2 * n_src:]
+    out_ref, tok, side, normed, qs, kv, mix, inside, wq, wk, wv, wo, sems = rest[2 * n_src:]
     key_rows, breadth, channels = tok.shape
     wide = normed.shape[1]
     rows = ROWS * len(spans)
@@ -55,7 +56,7 @@
     ]
     for c in copies + weights:
         c.start()
-    gain = gains_ref[0:1, :]
+    gain = gain_ref[...].reshape(1, -1)
     normed[:, breadth:, :] = jnp.zeros((key_rows, wide - breadth, channels), jnp.float32)
     n = lax.broadcasted_iota(jnp.int32, (1, SPAN * KC), 1)
     key_row = (n * 2731) >> 16
@@ -83,24 +84,27 @@
     kv[:, :, :channels] = jnp.dot(flat, wk[...], preferred_element_type=jnp.float32).reshape(key_rows, wide, channels)
     kv[:, :, channels:] = jnp.dot(flat, wv[...], preferred_element_type=jnp.float32).reshape(key_rows, wide, channels)
 
-    for n_span, (first_row, key0) in enumerate(spans):
+    for n_span, (first_row, _) in enumerate(spans):
         row_at = key_row + (row0 + first_row - 3)
-        inside = jnp.where(near & (row_at >= 0) & (row_at < height), 0.0, -jnp.inf)
-        own, keys = slice(n_span * ROWS, n_span * ROWS + ROWS), slice(key0, key0 + SPAN)
-
-        def block(cb, carry):
-            c0 = pl.multiple_of(cb * QC, QC)
-            col_at = key_col + (col0 + c0 - 3)
-            bias = inside + jnp.where((col_at >= 0) & (col_at < width), 0.0, -jnp.inf)
-            for l0, l1 in ((0, 256), (256, 384)):
-                qp = qs[own, pl.ds(c0, QC), l0:l1].reshape(ROWS * QC, l1 - l0)
-                kp = kv[keys, pl.ds(c0, KC), l0:l1].reshape(SPAN * KC, l1 - l0).astype(jnp.bfloat16)
-                vp = kv[keys, pl.ds(c0, KC), channels + l0:channels + l1].reshape(SPAN * KC, l1 - l0).astype(jnp.bfloat16)
-                mixed = attend_heads(qp, kp, vp, bias)
-                mix[own, pl.ds(c0, QC), l0:l1] = mixed.astype(jnp.bfloat16).reshape(ROWS, QC, l1 - l0)
-            return carry
-
-        lax.fori_loop(0, breadth // QC, block, 0, unroll=4)
+        inside[n_span] = jnp.where(near & (row_at >= 0) & (row_at < height), 0.0, -jnp.inf)
+    per_span = breadth // QC
+    key_step = spans[1][1]
+
+    def block(n, carry):
+        span, cb = lax.div(n, per_span), lax.rem(n, per_span)
+        own, keys = pl.ds(span * ROWS, ROWS), pl.ds(span * key_step, SPAN)
+        c0 = pl.multiple_of(cb * QC, QC)
+        col_at = key_col + (col0 + c0 - 3)
+        bias = inside[span] + jnp.where((col_at >= 0) & (col_at < width), 0.0, -jnp.inf)
+        for l0, l1 in ((0, 256), (256, 384)):
+            qp = qs[own, pl.ds(c0, QC), l0:l1].reshape(ROWS * QC, l1 - l0)
+            kp = kv[keys, pl.ds(c0, KC), l0:l1].reshape(SPAN * KC, l1 - l0).astype(jnp.bfloat16)
+            vp = kv[keys, pl.ds(c0, KC), channels + l0:channels + l1].reshape(SPAN * KC, l1 - l0).astype(jnp.bfloat16)
+            mixed = attend_heads(qp, kp, vp, bias)
+            mix[own, pl.ds(c0, QC), l0:l1] = mixed.astype(jnp.bfloat16).reshape(ROWS, QC, l1 - l0)
+        return carry
+
+    lax.fori_loop(0, len(spans) * per_span, block, 0, unroll=8)
     out = jnp.dot(mix[...].reshape(rows * breadth, channels), wo[...], preferred_element_type=jnp.float32)
     base = jnp.concatenate([tok[key0 + 3:key0 + 3 + ROWS] for _, key0 in spans], axis=0)
     out_ref[...] = (base.astype(jnp.float32).reshape(rows * breadth, channels) + out).astype(jnp.bfloat16)
@@ -129,6 +133,7 @@
             pltpu.VMEM((rows, breadth, channels), jnp.bfloat16),
             pltpu.VMEM((at, wide, 2 * channels), jnp.float32),
             pltpu.VMEM((rows, breadth, channels), jnp.bfloat16),
+            pltpu.VMEM((len(spans), ROWS * QC, SPAN * KC), jnp.float32),
             square, square, square, square,
             pltpu.SemaphoreType.DMA((4 + 2 * len(srcs),)),
         ],
@@ -139,6 +144,7 @@
 
 TILE = 16
 PART = 64
+BATCH = 4
 RIM = 2
 SIDE = 8
 PIECE = 512
@@ -146,7 +152,7 @@
 def gather_kernel(plan, n_arrays, piece_rows, *refs):
     place_ref, gains_ref, idx_hbm, w_hbm, qa_hbm, ta_hbm, wk_hbm, wv_hbm, wo_hbm = refs[:9]
     arrays = refs[9:9 + n_arrays]
-    (joined_ref, normed_ref, top_ref, bottom_ref, edge_ref, table, res, keys, values, mix,
+    (joined_ref, normed_ref, top_ref, bottom_ref, edge_ref, table, res, mix,
      idx_ref, w_ref, qa_ref, ta_ref, wk_ref, wv_ref, wo_ref, stage, sems, stage_sems) = refs[9 + n_arrays:]
     copies = [
         pltpu.make_async_copy(src, dst, sems.at[n])
@@ -184,54 +190,54 @@
 
     idx1, w1 = idx_ref.reshape(4 * total), w_ref.reshape(4 * total)
 
-    def line(n, carry):
-        row, col = lax.rem(n, TILE), lax.div(n, TILE) * TILE
-        at0 = n * (TILE * lanes)
+    def line(tile, i):
+        at0 = tile * (rows * lanes) + i * (TILE * lanes)
+        base = i * breadth + tile * TILE
         for j in range(TILE):
             acc = None
             for k in range(4):
-                at = k * total + row * breadth + col + j
+                at = base + (k * total + j)
                 term = w1[at] * flat[pl.ds(idx1[at], lanes, stride=8), :]
                 acc = term if acc is None else acc + term
             out[pl.ds(at0 + (j // 8) * (8 * lanes) + j % 8, lanes, stride=8), :] = acc
+
+    def first_tile(i, carry):
+        line(0, i)
         return carry
 
-    lax.fori_loop(0, tiles * TILE, line, 0)
+    lax.fori_loop(0, TILE, first_tile, 0)
     for c in copies[2:]:
         c.wait()
 
-    def project(t, carry):
+    def attend(t, carry):
         r = jnp.concatenate([res[pl.ds(t * (rows // 8), rows // 8), j].reshape(rows, 128) for j in range(lanes)], axis=1)
         nr = rms_rows(r.astype(jnp.bfloat16).astype(jnp.float32), gains_ref[2:3, :]).astype(jnp.bfloat16)
-        at = pl.ds(pl.multiple_of(t * rows, rows), rows)
-        keys[at, :] = jnp.dot(nr, wk_ref[...], preferred_element_type=jnp.float32).astype(jnp.bfloat16)
-        values[at, :] = jnp.dot(nr, wv_ref[...], preferred_element_type=jnp.float32).astype(jnp.bfloat16)
+        kk = jnp.dot(nr, wk_ref[...], preferred_element_type=jnp.float32).astype(jnp.bfloat16)
+        vv = jnp.dot(nr, wv_ref[...], preferred_element_type=jnp.float32).astype(jnp.bfloat16)
+        qa = qa_ref[:, pl.ds(pl.multiple_of(t * TILE, TILE), TILE), :].reshape(rows, channels)
+        following = jnp.minimum(t + 1, tiles - 1)
+        units = [(l0, l1, q0) for l0, l1 in ((0, 256), (256, 384)) for q0 in range(0, rows, PART)]
+        per = TILE // len(units)
+        for n, (l0, l1, q0) in enumerate(units):
+            mixed = attend_heads(qa[q0:q0 + PART, l0:l1], kk[:, l0:l1], vv[:, l0:l1], None)
+            mix[pl.ds(pl.multiple_of(t * rows + q0, PART), PART), l0:l1] = mixed.astype(jnp.bfloat16)
+            for i in range(n * per, n * per + per):
+                line(following, i)
         return carry
 
-    lax.fori_loop(0, tiles, project, 0, unroll=2)
-
-    def attend(t, carry):
-        at = pl.ds(pl.multiple_of(t * rows, rows), rows)
-        qa = qa_ref[:, pl.ds(pl.multiple_of(t * TILE, TILE), TILE), :].reshape(rows, channels)
-        for l0, l1 in ((0, 256), (256, 384)):
-            kp, vp = keys[at, l0:l1], values[at, l0:l1]
-            for q0 in range(0, rows, PART):
-                mixed = attend_heads(qa[q0:q0 + PART, l0:l1], kp, vp, None)
-                mix[pl.ds(pl.multiple_of(t * rows + q0, PART), PART), l0:l1] = mixed.astype(jnp.bfloat16)
+    lax.fori_loop(0, tiles, attend, 0)
+
+    def finish(t, carry):
+        at = pl.ds(pl.multiple_of(t * (BATCH * rows), rows), BATCH * rows)
+        o = jnp.dot(mix[at, :], wo_ref[...], preferred_element_type=jnp.float32)
+        for n in range(BATCH):
+            cols = pl.ds(pl.multiple_of((t * BATCH + n) * TILE, TILE), TILE)
+            joined = (ta_ref[:, cols, :].reshape(rows, channels).astype(jnp.float32) + o[n * rows:(n + 1) * rows]).astype(jnp.bfloat16)
+            joined_ref[:, cols, :] = joined.reshape(TILE, TILE, channels)
+            normed_ref[:, cols, :] = rms_rows(joined.astype(jnp.float32), gains_ref[3:4, :]).astype(jnp.bfloat16).reshape(TILE, TILE, channels)
         return carry
 
-    lax.fori_loop(0, tiles, attend, 0, unroll=2)
-
-    def finish(t, carry):
-        at = pl.ds(pl.multiple_of(t * rows, rows), rows)
-        cols = pl.ds(pl.multiple_of(t * TILE, TILE), TILE)
-        o = jnp.dot(mix[at, :], wo_ref[...], preferred_element_type=jnp.float32)
-        joined = (ta_ref[:, cols, :].reshape(rows, channels).astype(jnp.float32) + o).astype(jnp.bfloat16)
-        joined_ref[:, cols, :] = joined.reshape(TILE, TILE, channels)
-        normed_ref[:, cols, :] = rms_rows(joined.astype(jnp.float32), gains_ref[3:4, :]).astype(jnp.bfloat16).reshape(TILE, TILE, channels)
-        return carry
-
-    lax.fori_loop(0, tiles, finish, 0, unroll=2)
+    lax.fori_loop(0, tiles // BATCH, finish, 0)
     top_ref[...] = normed_ref[0:RIM]
     bottom_ref[...] = normed_ref[height - RIM:height]
     first_group = place_ref[1] == 0
@@ -263,8 +269,6 @@
         scratch_shapes=[
             pltpu.VMEM((n * piece_rows // 8, lanes, 8, 128), jnp.float32),
             pltpu.VMEM((total // 8, lanes, 8, 128), jnp.float32),
-            pltpu.VMEM((total, channels), jnp.bfloat16),
-            pltpu.VMEM((total, channels), jnp.bfloat16),
             pltpu.VMEM((total, channels), jnp.bfloat16),
             pltpu.SMEM(idx.shape, jnp.int32),
             pltpu.SMEM(idx.shape, jnp.float32),
@@ -565,8 +569,6 @@
         swath * height, group * breadth, jnp.int32(whole[0]), jnp.int32(whole[1]),
         swath, group, jnp.int32(groups), jnp.int32(cap), jnp.int32(height * breadth),
     ]).astype(jnp.int32)
-    row = lax.broadcasted_iota(jnp.int32, (8, channels), 0)
-    gains = sum(jnp.where(row == n, gain[None, :], 0.0) for n, gain in enumerate((swath_gain, query_gain, source_gain, conv_gain)))
 
     margin = 3
     side = lax.ppermute(inner_edge(tokens_b), "group", swap)
@@ -581,12 +583,14 @@
         return lax.ppermute(rows, "swath", relay)
 
     r0, r1, r2, r3 = range(0, height, ROWS)
-    middle = window_call(place, gains, *projections, ((r1, 0), (r2, ROWS)), [(tokens_b, side, r1 - margin, r1 - margin, SPAN + ROWS)])
+    middle = window_call(place, swath_gain, *projections, ((r1, 0), (r2, ROWS)), [(tokens_b, side, r1 - margin, r1 - margin, SPAN + ROWS)])
     near_middle = near(middle)
+    row = lax.broadcasted_iota(jnp.int32, (8, channels), 0)
+    gains = sum(jnp.where(row == n, gain[None, :], 0.0) for n, gain in enumerate((swath_gain, query_gain, source_gain, after(conv_gain, middle))))
     rims = after(jnp.concatenate([top, bottom], axis=0), middle)
     rims = lax.ppermute(inner_edge(rims), "group", swap)
     ends = window_call(
-        after(place, middle), gains, *projections, ((r0, 0), (r3, SPAN)),
+        after(place, middle), swath_gain, *projections, ((r0, 0), (r3, SPAN)),
         [(top, rims, 0, 0, margin), (tokens_b, side, 0, 0, SPAN - margin),
          (tokens_b, side, r3 - margin, r3 - margin, SPAN - margin), (bottom, rims, 0, margin, margin)],
     )

time: 150 us -> 145 us (0.967)
  Pallas kernels: 86.6 us -> 82.3 us
    pallas_call x1, Pallas kernels: 29.7 us -> 26.2 us  [gather_call(): pl.pallas_call(functools.partial(gather_kernel, tuple(plan), len(arrays),...]
    unnamed x38 -> x46, local copies, waits for them, and re-layouts: 3.83 us -> 3.87 us
  transfers between devices with their start and end apart: 21 -> 21, of which waited for: 5 -> 5; matrix products, arithmetic and copies ran while one was open for 3% -> 2% of each run, Pallas kernels for 34% -> 34%
where the time goes in v1:
time: 145 us; the launch traced here: 144 us
  Pallas kernels  82.3 us (57%)
  starting transfers between devices  36.4 us (25%)
  waiting for transfers between devices  17.1 us (12%)
  local copies, waits for them, and re-layouts  7.31 us (5%)
    pallas_call x2, Pallas kernels, window_call(): pl.pallas_call(functools.partial(window_kernel, tuple(spans), tuple(plan)...  27.2 us
    pallas_call x1, Pallas kernels, gather_call(): pl.pallas_call(functools.partial(gather_kernel, tuple(plan), len(arrays),...  26.2 us
    ppermute x2, waiting for transfers between devices, near(): return lax.ppermute(rows, 'swath', pairs)  12.8 us
    pallas_call x1, Pallas kernels, first_call(): pl.pallas_call(functools.partial(first_kernel, STEP1), out_shape=jax.Shap...  9.03 us
    pallas_call x1, Pallas kernels, second_call(): pl.pallas_call(functools.partial(second_kernel, STEP2), out_shape=jax.Sha...  7.56 us
    pallas_call x1, Pallas kernels, rim_call(): pl.pallas_call(rim_kernel, out_shape=jax.ShapeDtypeStruct(joined.shape, j...  6.76 us
    ppermute x2, starting transfers between devices, far(): return lax.ppermute(rows, 'swath', relay)  6.61 us
    ppermute x6, starting transfers between devices, body(): swapped = lambda rows: lax.ppermute(rows, 'group', swap)  5.27 us
  transfers between devices with their start and end apart: 21, of which 5 were waited for; matrix products, arithmetic and copies ran while one was open for 2% of the time, Pallas kernels for 34%

profile of v1, /device:TPU:11, one launch (start us, length us, event | category | flops | bytes accessed | tf_op | source)
XLA Modules:
  0.0 144.0 jit_solution(4093050693749335696)
XLA Ops:
  0.0 0.9 constant_dynamic-slice_fusion.2
  0.9 0.7 collective-permute-start
  1.6 1.1 fusion
  2.8 3.0 %collective-permute-start.2 = (bf16[3,128,384]{2,1,0:T(8,128)(2,1)S(1)}, bf16[3,128,384]{2,1,0:T(8,128)(2,1)S(1)}, u32[]{:S(2)}, u32[]{:S(2)}) collective-permute-start(bf16[3,128,384]{2,1,0:T(8,128)(2,1)S(1)} %get-tuple-element.45), channel_id=1, source_target_pairs={{2,0},{4,2},{6,4},{8,6},{10,8},{12,10},{14,12},{3,1},{5,3},{7,5},{... | collective-permute-start | bytes 884744 | tf_op jit(solution)/shard_map/ppermute | solution.py:576
  5.8 2.2 %collective-permute-start.1 = (bf16[3,128,384]{2,1,0:T(8,128)(2,1)S(1)}, bf16[3,128,384]{2,1,0:T(8,128)(2,1)S(1)}, u32[]{:S(2)}, u32[]{:S(2)}) collective-permute-start(bf16[3,128,384]{2,1,0:T(8,128)(2,1)S(1)} %get-tuple-element.46), channel_id=1, source_target_pairs={{0,2},{2,4},{4,6},{6,8},{8,10},{10,12},{12,14},{1,3},{3,5},{5,7},{... | collective-permute-start | bytes 884744 | tf_op jit(solution)/shard_map/ppermute | solution.py:575
  8.1 0.7 stack.19.place_ref.refs_0_
  8.8 0.0 collective-permute-done.rest_1_.rest_5_.rest_6_
  8.8 0.6 copy-done.21
  9.4 13.1 %shard_map.190.refs_10_ = bf16[1024,384]{1,0:T(8,128)(2,1)} custom-call(s32[9]{0:T(128)} %stack.19.place_ref.refs_0_, f32[384]{0:T(512)} %gain_ref.3, bf16[384,384]{1,0:T(8,128)(2,1)} %wq_hbm.3, bf16[384,384]{1,0:T(8,128)(2,1)} %wk_hbm.3, bf16[384,384]{1,0:T(8,128)(2,1)} %wv_hbm.3, bf16[384,384]{1,0:T(8,128)(2,1)} %wo_hbm.3, bf16[16,128,384]{2,1,0:T(8,128)(2,1)} %rest_2_.1, ...), custom_call_target="tpu_custom_call" | custom-call | flops 14000000000 | bytes 4000000 | tf_op jit(solution)/shard_map/pallas_call | solution.py:123
  22.5 0.0 collective-permute-done.2.rest_3_
  22.6 0.0 collective-permute-done.1.rest_0_
  22.6 0.0 copy-start.11
  22.6 0.1 pad_maximum_fusion
  22.7 0.0 copy-start.15
  22.7 0.0 copy-start.16
  22.7 0.0 copy-start.17
  22.7 0.0 copy-start.18
  22.7 0.0 copy-start
  22.8 0.0 copy-start.2
  22.8 0.6 collective-permute-start.3
  23.4 2.2 %collective-permute-start.10 = (bf16[1024,384]{1,0:T(8,128)(2,1)}, bf16[1024,384]{1,0:T(8,128)(2,1)}, u32[]{:S(2)}, u32[]{:S(2)}) collective-permute-start(bf16[1024,384]{1,0:T(8,128)(2,1)} %shard_map.190.refs_10_), channel_id=1, source_target_pairs={{0,2},{2,0},{4,6},{6,4},{8,10},{10,8},{12,14},{14,12},{1,3},{3,1},... | collective-permute-start | bytes 2359304 | tf_op jit(solution)/shard_map/ppermute | solution.py:580
  25.6 0.0 collective-permute-done.3.rest_4_.rest_7_
  25.6 0.6 copy-done.22
  26.2 14.0 %shard_map.191.refs_9_ = bf16[1024,384]{1,0:T(8,128)(2,1)} custom-call(s32[9]{0:T(128)} %stack.19.place_ref.refs_0_, f32[384]{0:T(512)} %gain_ref.3, bf16[384,384]{1,0:T(8,128)(2,1)} %wq_hbm.3, bf16[384,384]{1,0:T(8,128)(2,1)} %wk_hbm.3, bf16[384,384]{1,0:T(8,128)(2,1)} %wv_hbm.3, bf16[384,384]{1,0:T(8,128)(2,1)} %wo_hbm.3, bf16[3,128,384]{2,1,0:T(8,128)(2,1)} %copy-done.11, ...), custom_call_target="tpu_custom_call" | custom-call | flops 14000000000 | bytes 4000000 | tf_op jit(solution)/shard_map/pallas_call | solution.py:123
  40.2 0.9 collective-permute-start.4
  41.2 0.7 collective-permute-start.9
  41.9 0.1 select_add_fusion.gains_ref.refs_1_
  41.9 1.8 %collective-permute-done.10.refs_14_ = bf16[1024,384]{1,0:T(8,128)(2,1)} collective-permute-done((bf16[1024,384]{1,0:T(8,128)(2,1)}, bf16[1024,384]{1,0:T(8,128)(2,1)}, u32[]{:S(2)}, u32[]{:S(2)}) %collective-permute-start.10) | collective-permute-done | bytes 786464 | tf_op jit(solution)/shard_map/ppermute | solution.py:580
  43.7 3.4 %collective-permute-start.14 = (bf16[1024,384]{1,0:T(8,128)(2,1)}, bf16[1024,384]{1,0:T(8,128)(2,1)}, u32[]{:S(2)}, u32[]{:S(2)}) collective-permute-start(bf16[1024,384]{1,0:T(8,128)(2,1)} %collective-permute-done.10.refs_14_), channel_id=1, source_target_pairs={{0,4},{4,8},{6,2},{8,12},{10,6},{14,10},{1,5},{5,9},{7,3},{9,13},{... | collective-permute-start | bytes 2359304 | tf_op jit(solution)/shard_map/ppermute | solution.py:583
  47.1 1.2 shard_map.194.refs_4_
  48.4 0.0 copy-start.1
  48.4 1.1 copy-done.1
  49.5 11.0 %collective-permute-done.4.refs_13_ = bf16[1024,384]{1,0:T(8,128)(2,1)} collective-permute-done((bf16[1024,384]{1,0:T(8,128)(2,1)}, bf16[1024,384]{1,0:T(8,128)(2,1)}, u32[]{:S(2)}, u32[]{:S(2)}) %collective-permute-start.4) | collective-permute-done | bytes 786464 | tf_op jit(solution)/shard_map/ppermute | solution.py:580
  60.6 3.2 %collective-permute-start.13 = (bf16[1024,384]{1,0:T(8,128)(2,1)}, bf16[1024,384]{1,0:T(8,128)(2,1)}, u32[]{:S(2)}, u32[]{:S(2)}) collective-permute-start(bf16[1024,384]{1,0:T(8,128)(2,1)} %collective-permute-done.4.refs_13_), channel_id=1, source_target_pairs={{0,4},{4,8},{6,2},{8,12},{10,6},{14,10},{1,5},{5,9},{7,3},{9,13},{... | collective-permute-start | bytes 2359304 | tf_op jit(solution)/shard_map/ppermute | solution.py:583
  63.8 1.5 %shard_map.192 = (s32[3,9,128]{2,1,0:T(8,128)}, s32[3,9,128]{2,1,0:T(8,128)}) custom-call(s32[9]{0:T(128)} %stack.19.place_ref.refs_0_, s32[16,1024]{1,0:T(8,128)} %bitcast.8, s32[1,16]{1,0:T(1,128)} %bitcast.11), custom_call_target="tpu_custom_call" | custom-call | flops 1000000 | bytes 100000 | tf_op jit(solution)/shard_map/pallas_call | solution.py:465
  65.3 0.9 collective-permute-start.5
  66.2 0.7 fusion.1
  66.9 0.3 collective-permute-done.5.taken_ref
  67.3 2.3 %collective-permute-start.6 = (s32[2,9,128]{2,1,0:T(8,128)S(1)}, s32[2,9,128]{2,1,0:T(8,128)S(1)}, u32[]{:S(2)}, u32[]{:S(2)}) collective-permute-start(s32[2,9,128]{2,1,0:T(8,128)S(1)} %pad_add_fusion), channel_id=1, source_target_pairs={{0,2},{2,4},{4,6},{6,8},{8,10},{10,12},{12,14},{1,3},{3,5},{5,7},{... | collective-permute-start | bytes 27656 | tf_op jit(solution)/shard_map/ppermute | solution.py:602
  69.6 3.9 %collective-permute-start.7 = (s32[2,9,128]{2,1,0:T(8,128)S(1)}, s32[2,9,128]{2,1,0:T(8,128)S(1)}, u32[]{:S(2)}, u32[]{:S(2)}) collective-permute-start(s32[2,9,128]{2,1,0:T(8,128)S(1)} %pad_add_fusion.1), channel_id=1, source_target_pairs={{2,0},{4,2},{6,4},{8,6},{10,8},{12,10},{14,12},{3,1},{5,3},{7,5},{... | collective-permute-start | bytes 27656 | tf_op jit(solution)/shard_map/ppermute | solution.py:603
  73.5 1.0 collective-permute-start.8
  74.5 0.0 collective-permute-done.7.lower_ref
  74.5 1.3 collective-permute-start.12
  75.8 2.9 %shard_map.193 = (s32[64,128]{1,0:T(8,128)}, f32[64,128]{1,0:T(8,128)}) custom-call(s32[9]{0:T(128)} %stack.19.place_ref.refs_0_, s32[64,128]{1,0:T(8,128)} %bitcast.9, f32[64,128]{1,0:T(8,128)} %bitcast.10, s32[2,9,128]{2,1,0:T(8,128)} %copy-done.13, s32[3,9,128]{2,1,0:T(8,128)} %get-tuple-element.30.keep_ref, s32[3,9,128]{2,1,0:T(8,128)} %copy-done.12, ...), custom_call_target="tpu_custom_call" | custom-call | flops 1000000 | bytes 100000 | tf_op jit(solution)/shard_map/pallas_call | solution.py:499
  78.8 0.7 collective-permute-start.11
  79.4 0.1 collective-permute-start.16
  79.5 1.7 %collective-permute-done.13.refs_17_ = bf16[1024,384]{1,0:T(8,128)(2,1)} collective-permute-done((bf16[1024,384]{1,0:T(8,128)(2,1)}, bf16[1024,384]{1,0:T(8,128)(2,1)}, u32[]{:S(2)}, u32[]{:S(2)}) %collective-permute-start.13) | collective-permute-done | bytes 786464 | tf_op jit(solution)/shard_map/ppermute | solution.py:583
  81.2 1.5 %collective-permute-start.15 = (bf16[1024,384]{1,0:T(8,128)(2,1)}, bf16[1024,384]{1,0:T(8,128)(2,1)}, u32[]{:S(2)}, u32[]{:S(2)}) collective-permute-start(bf16[1024,384]{1,0:T(8,128)(2,1)} %collective-permute-done.13.refs_17_), channel_id=1, source_target_pairs={{0,1},{1,0},{2,3},{3,2},{4,5},{5,4},{6,7},{7,6},{8,9},{9,8},{10,11... | collective-permute-start | bytes 2359304 | tf_op jit(solution)/shard_map/ppermute | solution.py:613
  82.7 0.0 collective-permute-done.8.refs_11_
  82.7 0.0 collective-permute-done.12.refs_16_
  82.7 0.0 collective-permute-done.16.refs_20_
  82.7 2.2 %collective-permute-done.15.refs_19_ = bf16[1024,384]{1,0:T(8,128)(2,1)} collective-permute-done((bf16[1024,384]{1,0:T(8,128)(2,1)}, bf16[1024,384]{1,0:T(8,128)(2,1)}, u32[]{:S(2)}, u32[]{:S(2)}) %collective-permute-start.15) | collective-permute-done | bytes 786464 | tf_op jit(solution)/shard_map/ppermute | solution.py:613
  85.0 26.2 %shard_map.195 = (bf16[16,128,384]{2,1,0:T(8,128)(2,1)}, bf16[16,128,384]{2,1,0:T(8,128)(2,1)}, bf16[2,128,384]{2,1,0:T(8,128)(2,1)}, bf16[2,128,384]{2,1,0:T(8,128)(2,1)}, bf16[16,8,384]{2,1,0:T(8,128)(2,1)}) custom-call(s32[9]{0:T(128)} %stack.19.place_ref.refs_0_, f32[8,384]{1,0:T(8,128)} %copy-done.3, s32[64,128]{1,0:T(8,128)} %get-tuple-element.32.refs_2_, ...), custom_call_target="tpu_custom_call" | custom-call | flops 30000001024 | bytes 10000000 | tf_op jit(solution)/shard_map/pallas_call | solution.py:264
  111.2 0.4 collective-permute-start.17
  111.6 3.2 %collective-permute-start.18 = (bf16[2,128,384]{2,1,0:T(8,128)(2,1)}, bf16[2,128,384]{2,1,0:T(8,128)(2,1)S(1)}, u32[]{:S(2)}, u32[]{:S(2)}) collective-permute-start(bf16[2,128,384]{2,1,0:T(8,128)(2,1)} %get-tuple-element.41), channel_id=1, source_target_pairs={{0,2},{2,4},{4,6},{6,8},{8,10},{10,12},{12,14},{1,3},{3,5},{5,7},{... | collective-permute-start | bytes 589832 | tf_op jit(solution)/shard_map/ppermute | solution.py:626
  114.8 3.2 %collective-permute-start.19 = (bf16[2,128,384]{2,1,0:T(8,128)(2,1)}, bf16[2,128,384]{2,1,0:T(8,128)(2,1)S(1)}, u32[]{:S(2)}, u32[]{:S(2)}) collective-permute-start(bf16[2,128,384]{2,1,0:T(8,128)(2,1)} %get-tuple-element.42), channel_id=1, source_target_pairs={{2,0},{4,2},{6,4},{8,6},{10,8},{12,10},{14,12},{3,1},{5,3},{7,5},{... | collective-permute-start | bytes 589832 | tf_op jit(solution)/shard_map/ppermute | solution.py:627
  118.0 0.0 collective-permute-done.17.side_ref
  118.1 1.4 copy-done.8
  119.5 9.0 %shard_map.196.inner_ref = bf16[14,144,384]{2,1,0:T(8,128)(2,1)S(1)} custom-call(s32[9]{0:T(128)S(1)} %copy-done.4, bf16[16,128,384]{2,1,0:T(8,128)(2,1)S(1)} %copy-done.8, bf16[16,8,384]{2,1,0:T(8,128)(2,1)S(1)} %collective-permute-done.17.side_ref, bf16[3,3,384,384]{3,2,1,0:T(8,128)(2,1)S(1)} %copy-done.5), custom_call_target="tpu_custom_call" | custom-call | flops 10000000000 | bytes 4000000 | tf_op jit(solution)/shard_map/pallas_call | solution.py:399
  128.5 0.0 collective-permute-done.18.top_ref
  128.6 0.8 collective-permute-start.20
  129.4 7.6 %shard_map.197.merged_hbm = bf16[16,128,384]{2,1,0:T(8,128)(2,1)} custom-call(bf16[14,144,384]{2,1,0:T(8,128)(2,1)S(1)} %shard_map.196.inner_ref, bf16[16,128,384]{2,1,0:T(8,128)(2,1)S(1)} %copy-done.7, bf16[3,3,384,384]{3,2,1,0:T(8,128)(2,1)S(1)} %copy-done.6), custom_call_target="tpu_custom_call" | custom-call | flops 8000000000 | bytes 4000000 | tf_op jit(solution)/shard_map/pallas_call | solution.py:415
  137.0 0.0 collective-permute-done.20.side_rim_ref
  137.0 6.8 %shard_map.198 = bf16[16,128,384]{2,1,0:T(8,128)(2,1)} custom-call(s32[9]{0:T(128)S(1)} %copy-done.4, bf16[16,128,384]{2,1,0:T(8,128)(2,1)S(1)} %copy-done.9, bf16[16,8,384]{2,1,0:T(8,128)(2,1)S(1)} %collective-permute-done.17.side_ref, bf16[2,128,384]{2,1,0:T(8,128)(2,1)S(1)} %collective-permute-done.18.top_ref, ...), custom_call_target="tpu_custom_call", output_to_operand_aliasing={{}: (10, {})} | custom-call | flops 5000000000 | bytes 4000000 | tf_op jit(solution)/shard_map/pallas_call | solution.py:428
  (47 shorter events, 0.2 us)
Async XLA Ops:
  0.9 7.9 %collective-permute-start = (bf16[16,8,384]{2,1,0:T(8,128)(2,1)S(1)}, bf16[16,8,384]{2,1,0:T(8,128)(2,1)S(1)}, u32[]{:S(2)}, u32[]{:S(2)}) collective-permute-start(bf16[16,8,384]{2,1,0:T(8,128)(2,1)S(1)} %constant_dynamic-slice_fusion.2), channel_id=1, source_target_pairs={{0,1},{1,0},{2,3},{3,2},{4,5},{5,4},{6,7},{7,6},{8,9},{9,8},{10,11... | collective-permute-start | bytes 294920 | tf_op jit(solution)/shard_map/ppermute | solution.py:574
  2.8 19.8 %collective-permute-start.2 = (bf16[3,128,384]{2,1,0:T(8,128)(2,1)S(1)}, bf16[3,128,384]{2,1,0:T(8,128)(2,1)S(1)}, u32[]{:S(2)}, u32[]{:S(2)}) collective-permute-start(bf16[3,128,384]{2,1,0:T(8,128)(2,1)S(1)} %get-tuple-element.45), channel_id=1, source_target_pairs={{2,0},{4,2},{6,4},{8,6},{10,8},{12,10},{14,12},{3,1},{5,3},{7,5},{... | collective-permute-start | bytes 884744 | tf_op jit(solution)/shard_map/ppermute | solution.py:576
  5.8 16.8 %collective-permute-start.1 = (bf16[3,128,384]{2,1,0:T(8,128)(2,1)S(1)}, bf16[3,128,384]{2,1,0:T(8,128)(2,1)S(1)}, u32[]{:S(2)}, u32[]{:S(2)}) collective-permute-start(bf16[3,128,384]{2,1,0:T(8,128)(2,1)S(1)} %get-tuple-element.46), channel_id=1, source_target_pairs={{0,2},{2,4},{4,6},{6,8},{8,10},{10,12},{12,14},{1,3},{3,5},{5,7},{... | collective-permute-start | bytes 884744 | tf_op jit(solution)/shard_map/ppermute | solution.py:575
  8.8 0.6 copy-start.21
  22.6 3.0 %copy-start.10 = (bf16[3,128,384]{2,1,0:T(8,128)(2,1)}, bf16[3,128,384]{2,1,0:T(8,128)(2,1)S(1)}, u32[]{:S(2)}) copy-start(bf16[3,128,384]{2,1,0:T(8,128)(2,1)S(1)} %collective-permute-done.2.rest_3_) | copy-start | bytes 884740
  22.6 3.0 %copy-start.11 = (bf16[3,128,384]{2,1,0:T(8,128)(2,1)}, bf16[3,128,384]{2,1,0:T(8,128)(2,1)S(1)}, u32[]{:S(2)}) copy-start(bf16[3,128,384]{2,1,0:T(8,128)(2,1)S(1)} %collective-permute-done.1.rest_0_) | copy-start | bytes 884740
  22.7 18.5 %copy-start.19 = (bf16[1024,384]{1,0:T(8,128)(2,1)S(1)}, bf16[1024,384]{1,0:T(8,128)(2,1)}, u32[]{:S(2)}) copy-start(bf16[1024,384]{1,0:T(8,128)(2,1)} %shard_map.190.refs_10_) | copy-start | bytes 2359300
  22.7 19.2 %copy-start.15 = (f32[384]{0:T(512)S(1)}, f32[384]{0:T(512)}, u32[]{:S(2)}) copy-start(f32[384]{0:T(512)} %param.37) | copy-start | bytes 4612
  22.7 19.1 %copy-start.16 = (f32[384]{0:T(512)S(1)}, f32[384]{0:T(512)}, u32[]{:S(2)}) copy-start(f32[384]{0:T(512)} %param.32) | copy-start | bytes 4612
  22.7 19.1 %copy-start.17 = (f32[384]{0:T(512)S(1)}, f32[384]{0:T(512)}, u32[]{:S(2)}) copy-start(f32[384]{0:T(512)} %param.31) | copy-start | bytes 4612
  22.7 19.1 %copy-start.18 = (f32[384]{0:T(512)S(1)}, f32[384]{0:T(512)}, u32[]{:S(2)}) copy-start(f32[384]{0:T(512)} %gain_ref.3) | copy-start | bytes 4612
  22.7 24.4 %copy-start = (bf16[16,128,384]{2,1,0:T(8,128)(2,1)S(1)}, bf16[16,128,384]{2,1,0:T(8,128)(2,1)}, u32[]{:S(2)}) copy-start(bf16[16,128,384]{2,1,0:T(8,128)(2,1)} %refs_5_) | copy-start | bytes 4718596
  22.8 24.4 %copy-start.2 = (bf16[384,384]{1,0:T(8,128)(2,1)S(1)}, bf16[384,384]{1,0:T(8,128)(2,1)}, u32[]{:S(2)}) copy-start(bf16[384,384]{1,0:T(8,128)(2,1)} %w_ref.1) | copy-start | bytes 884740
  22.8 2.8 %collective-permute-start.3 = (bf16[6,8,384]{2,1,0:T(8,128)(2,1)S(1)}, bf16[6,8,384]{2,1,0:T(8,128)(2,1)S(1)}, u32[]{:S(2)}, u32[]{:S(2)}) collective-permute-start(bf16[6,8,384]{2,1,0:T(8,128)(2,1)S(1)} %constant_dynamic-slice_fusion.1), channel_id=1, source_target_pairs={{0,1},{1,0},{2,3},{3,2},{4,5},{5,4},{6,7},{7,6},{8,9},{9,8},{10,11... | collective-permute-start | bytes 110600 | tf_op jit(solution)/shard_map/ppermute | solution.py:591
  23.4 20.3 %collective-permute-start.10 = (bf16[1024,384]{1,0:T(8,128)(2,1)}, bf16[1024,384]{1,0:T(8,128)(2,1)}, u32[]{:S(2)}, u32[]{:S(2)}) collective-permute-start(bf16[1024,384]{1,0:T(8,128)(2,1)} %shard_map.190.refs_10_), channel_id=1, source_target_pairs={{0,2},{2,0},{4,6},{6,4},{8,10},{10,8},{12,14},{14,12},{1,3},{3,1},... | collective-permute-start | bytes 2359304 | tf_op jit(solution)/shard_map/ppermute | solution.py:580
  25.6 0.6 copy-start.22
  40.2 20.3 %collective-permute-start.4 = (bf16[1024,384]{1,0:T(8,128)(2,1)}, bf16[1024,384]{1,0:T(8,128)(2,1)}, u32[]{:S(2)}, u32[]{:S(2)}) collective-permute-start(bf16[1024,384]{1,0:T(8,128)(2,1)} %shard_map.191.refs_9_), channel_id=1, source_target_pairs={{0,2},{2,0},{4,6},{6,4},{8,10},{10,8},{12,14},{14,12},{1,3},{3,1},... | collective-permute-start | bytes 2359304 | tf_op jit(solution)/shard_map/ppermute | solution.py:580
  41.2 38.3 %collective-permute-start.9 = (bf16[1024,384]{1,0:T(8,128)(2,1)S(1)}, bf16[1024,384]{1,0:T(8,128)(2,1)}, u32[]{:S(2)}, u32[]{:S(2)}) collective-permute-start(bf16[1024,384]{1,0:T(8,128)(2,1)S(1)} %copy-done.19), channel_id=1, source_target_pairs={{0,1},{1,0},{2,3},{3,2},{4,5},{5,4},{6,7},{7,6},{8,9},{9,8},{10,11... | collective-permute-start | bytes 2359304 | tf_op jit(solution)/shard_map/ppermute | solution.py:613
  41.9 6.4 %copy-start.3 = (f32[8,384]{1,0:T(8,128)}, f32[8,384]{1,0:T(8,128)S(1)}, u32[]{:S(2)}) copy-start(f32[8,384]{1,0:T(8,128)S(1)} %select_add_fusion.gains_ref.refs_1_) | copy-start | bytes 36868
  43.7 35.1 %collective-permute-start.14 = (bf16[1024,384]{1,0:T(8,128)(2,1)}, bf16[1024,384]{1,0:T(8,128)(2,1)}, u32[]{:S(2)}, u32[]{:S(2)}) collective-permute-start(bf16[1024,384]{1,0:T(8,128)(2,1)} %collective-permute-done.10.refs_14_), channel_id=1, source_target_pairs={{0,4},{4,8},{6,2},{8,12},{10,6},{14,10},{1,5},{5,9},{7,3},{9,13},{... | collective-permute-start | bytes 2359304 | tf_op jit(solution)/shard_map/ppermute | solution.py:583
  48.4 1.1 copy-start.1
  60.6 20.6 %collective-permute-start.13 = (bf16[1024,384]{1,0:T(8,128)(2,1)}, bf16[1024,384]{1,0:T(8,128)(2,1)}, u32[]{:S(2)}, u32[]{:S(2)}) collective-permute-start(bf16[1024,384]{1,0:T(8,128)(2,1)} %collective-permute-done.4.refs_13_), channel_id=1, source_target_pairs={{0,4},{4,8},{6,2},{8,12},{10,6},{14,10},{1,5},{5,9},{7,3},{9,13},{... | collective-permute-start | bytes 2359304 | tf_op jit(solution)/shard_map/ppermute | solution.py:583
  65.3 2.0 %collective-permute-start.5 = (s32[3,9,128]{2,1,0:T(8,128)}, s32[3,9,128]{2,1,0:T(8,128)S(1)}, u32[]{:S(2)}, u32[]{:S(2)}) collective-permute-start(s32[3,9,128]{2,1,0:T(8,128)} %get-tuple-element.31), channel_id=1, source_target_pairs={{0,1},{1,0},{2,3},{3,2},{4,5},{5,4},{6,7},{7,6},{8,9},{9,8},{10,11... | collective-permute-start | bytes 41480 | tf_op jit(solution)/shard_map/ppermute | solution.py:601
  67.3 8.6 %copy-start.12 = (s32[3,9,128]{2,1,0:T(8,128)}, s32[3,9,128]{2,1,0:T(8,128)S(1)}, u32[]{:S(2)}) copy-start(s32[3,9,128]{2,1,0:T(8,128)S(1)} %collective-permute-done.5.taken_ref) | copy-start | bytes 41476
  67.3 6.2 %collective-permute-start.6 = (s32[2,9,128]{2,1,0:T(8,128)S(1)}, s32[2,9,128]{2,1,0:T(8,128)S(1)}, u32[]{:S(2)}, u32[]{:S(2)}) collective-permute-start(s32[2,9,128]{2,1,0:T(8,128)S(1)} %pad_add_fusion), channel_id=1, source_target_pairs={{0,2},{2,4},{4,6},{6,8},{8,10},{10,12},{12,14},{1,3},{3,5},{5,7},{... | collective-permute-start | bytes 27656 | tf_op jit(solution)/shard_map/ppermute | solution.py:602
  69.6 4.9 %collective-permute-start.7 = (s32[2,9,128]{2,1,0:T(8,128)S(1)}, s32[2,9,128]{2,1,0:T(8,128)S(1)}, u32[]{:S(2)}, u32[]{:S(2)}) collective-permute-start(s32[2,9,128]{2,1,0:T(8,128)S(1)} %pad_add_fusion.1), channel_id=1, source_target_pairs={{2,0},{4,2},{6,4},{8,6},{10,8},{12,10},{14,12},{3,1},{5,3},{7,5},{... | collective-permute-start | bytes 27656 | tf_op jit(solution)/shard_map/ppermute | solution.py:603
  73.5 2.3 %copy-start.13 = (s32[2,9,128]{2,1,0:T(8,128)}, s32[2,9,128]{2,1,0:T(8,128)S(1)}, u32[]{:S(2)}) copy-start(s32[2,9,128]{2,1,0:T(8,128)S(1)} %collective-permute-done.6.upper_ref) | copy-start | bytes 27652
  73.5 9.2 %collective-permute-start.8 = (bf16[1024,384]{1,0:T(8,128)(2,1)}, bf16[1024,384]{1,0:T(8,128)(2,1)}, u32[]{:S(2)}, u32[]{:S(2)}) collective-permute-start(bf16[1024,384]{1,0:T(8,128)(2,1)} %shard_map.191.refs_9_), channel_id=1, source_target_pairs={{0,1},{1,0},{2,3},{3,2},{4,5},{5,4},{6,7},{7,6},{8,9},{9,8},{10,11... | collective-permute-start | bytes 2359304 | tf_op jit(solution)/shard_map/ppermute | solution.py:613
  74.5 1.3 copy-start.14
  74.5 8.2 %collective-permute-start.12 = (bf16[1024,384]{1,0:T(8,128)(2,1)}, bf16[1024,384]{1,0:T(8,128)(2,1)}, u32[]{:S(2)}, u32[]{:S(2)}) collective-permute-start(bf16[1024,384]{1,0:T(8,128)(2,1)} %collective-permute-done.10.refs_14_), channel_id=1, source_target_pairs={{0,1},{1,0},{2,3},{3,2},{4,5},{5,4},{6,7},{7,6},{8,9},{9,8},{10,11... | collective-permute-start | bytes 2359304 | tf_op jit(solution)/shard_map/ppermute | solution.py:613
  78.7 39.3 %copy-start.4 = (s32[9]{0:T(128)S(1)}, s32[9]{0:T(128)}, u32[]{:S(2)}) copy-start(s32[9]{0:T(128)} %stack.19.place_ref.refs_0_) | copy-start | bytes 112
  78.7 39.3 %copy-start.5 = (bf16[3,3,384,384]{3,2,1,0:T(8,128)(2,1)S(1)}, bf16[3,3,384,384]{3,2,1,0:T(8,128)(2,1)}, u32[]{:S(2)}) copy-start(bf16[3,3,384,384]{3,2,1,0:T(8,128)(2,1)} %w1_hbm.1) | copy-start | bytes 7962628
  78.8 4.0 %collective-permute-start.11 = (bf16[1024,384]{1,0:T(8,128)(2,1)}, bf16[1024,384]{1,0:T(8,128)(2,1)}, u32[]{:S(2)}, u32[]{:S(2)}) collective-permute-start(bf16[1024,384]{1,0:T(8,128)(2,1)} %collective-permute-done.4.refs_13_), channel_id=1, source_target_pairs={{0,1},{1,0},{2,3},{3,2},{4,5},{5,4},{6,7},{7,6},{8,9},{9,8},{10,11... | collective-permute-start | bytes 2359304 | tf_op jit(solution)/shard_map/ppermute | solution.py:613
  79.4 3.3 %collective-permute-start.16 = (bf16[1024,384]{1,0:T(8,128)(2,1)}, bf16[1024,384]{1,0:T(8,128)(2,1)S(1)}, u32[]{:S(2)}, u32[]{:S(2)}) collective-permute-start(bf16[1024,384]{1,0:T(8,128)(2,1)} %collective-permute-done.14.refs_18_), channel_id=1, source_target_pairs={{0,1},{1,0},{2,3},{3,2},{4,5},{5,4},{6,7},{7,6},{8,9},{9,8},{10,11... | collective-permute-start | bytes 2359304 | tf_op jit(solution)/shard_map/ppermute | solution.py:613
  81.2 3.8 %collective-permute-start.15 = (bf16[1024,384]{1,0:T(8,128)(2,1)}, bf16[1024,384]{1,0:T(8,128)(2,1)}, u32[]{:S(2)}, u32[]{:S(2)}) collective-permute-start(bf16[1024,384]{1,0:T(8,128)(2,1)} %collective-permute-done.13.refs_17_), channel_id=1, source_target_pairs={{0,1},{1,0},{2,3},{3,2},{4,5},{5,4},{6,7},{7,6},{8,9},{9,8},{10,11... | collective-permute-start | bytes 2359304 | tf_op jit(solution)/shard_map/ppermute | solution.py:613
  82.7 2.2 %copy-start.20 = (bf16[1024,384]{1,0:T(8,128)(2,1)}, bf16[1024,384]{1,0:T(8,128)(2,1)S(1)}, u32[]{:S(2)}) copy-start(bf16[1024,384]{1,0:T(8,128)(2,1)S(1)} %collective-permute-done.16.refs_20_) | copy-start | bytes 2359300
  111.2 6.9 %collective-permute-start.17 = (bf16[16,8,384]{2,1,0:T(8,128)(2,1)}, bf16[16,8,384]{2,1,0:T(8,128)(2,1)S(1)}, u32[]{:S(2)}, u32[]{:S(2)}) collective-permute-start(bf16[16,8,384]{2,1,0:T(8,128)(2,1)} %get-tuple-element.40), channel_id=1, source_target_pairs={{0,1},{1,0},{2,3},{3,2},{4,5},{5,4},{6,7},{7,6},{8,9},{9,8},{10,11... | collective-permute-start | bytes 294920 | tf_op jit(solution)/shard_map/ppermute | solution.py:625
  111.6 16.9 %collective-permute-start.18 = (bf16[2,128,384]{2,1,0:T(8,128)(2,1)}, bf16[2,128,384]{2,1,0:T(8,128)(2,1)S(1)}, u32[]{:S(2)}, u32[]{:S(2)}) collective-permute-start(bf16[2,128,384]{2,1,0:T(8,128)(2,1)} %get-tuple-element.41), channel_id=1, source_target_pairs={{0,2},{2,4},{4,6},{6,8},{8,10},{10,12},{12,14},{1,3},{3,5},{5,7},{... | collective-permute-start | bytes 589832 | tf_op jit(solution)/shard_map/ppermute | solution.py:626
  114.8 13.7 %collective-permute-start.19 = (bf16[2,128,384]{2,1,0:T(8,128)(2,1)}, bf16[2,128,384]{2,1,0:T(8,128)(2,1)S(1)}, u32[]{:S(2)}, u32[]{:S(2)}) collective-permute-start(bf16[2,128,384]{2,1,0:T(8,128)(2,1)} %get-tuple-element.42), channel_id=1, source_target_pairs={{2,0},{4,2},{6,4},{8,6},{10,8},{12,10},{14,12},{3,1},{5,3},{7,5},{... | collective-permute-start | bytes 589832 | tf_op jit(solution)/shard_map/ppermute | solution.py:627
  118.1 1.4 copy-start.8
  119.5 9.9 %copy-start.6 = (bf16[3,3,384,384]{3,2,1,0:T(8,128)(2,1)S(1)}, bf16[3,3,384,384]{3,2,1,0:T(8,128)(2,1)}, u32[]{:S(2)}) copy-start(bf16[3,3,384,384]{3,2,1,0:T(8,128)(2,1)} %w2_hbm.1) | copy-start | bytes 7962628
  119.5 9.9 %copy-start.7 = (bf16[16,128,384]{2,1,0:T(8,128)(2,1)S(1)}, bf16[16,128,384]{2,1,0:T(8,128)(2,1)}, u32[]{:S(2)}) copy-start(bf16[16,128,384]{2,1,0:T(8,128)(2,1)} %get-tuple-element.44.joined_ref) | copy-start | bytes 4718596
  128.6 8.4 %collective-permute-start.20 = (bf16[4,8,384]{2,1,0:T(8,128)(2,1)S(1)}, bf16[4,8,384]{2,1,0:T(8,128)(2,1)S(1)}, u32[]{:S(2)}, u32[]{:S(2)}) collective-permute-start(bf16[4,8,384]{2,1,0:T(8,128)(2,1)S(1)} %constant_dynamic-slice_fusion), channel_id=1, source_target_pairs={{0,1},{1,0},{2,3},{3,2},{4,5},{5,4},{6,7},{7,6},{8,9},{9,8},{10,11... | collective-permute-start | bytes 73736 | tf_op jit(solution)/shard_map/ppermute | solution.py:630
  129.4 7.6 %copy-start.9 = (bf16[16,128,384]{2,1,0:T(8,128)(2,1)S(1)}, bf16[16,128,384]{2,1,0:T(8,128)(2,1)}, u32[]{:S(2)}) copy-start(bf16[16,128,384]{2,1,0:T(8,128)(2,1)} %get-tuple-element.39.nc_ref) | copy-start | bytes 4718596

commit v2 on v1

--- a/solution.py
+++ b/solution.py
@@ -144,7 +144,6 @@
 
 TILE = 16
 PART = 64
-BATCH = 4
 RIM = 2
 SIDE = 8
 PIECE = 512
@@ -152,7 +151,7 @@
 def gather_kernel(plan, n_arrays, piece_rows, *refs):
     place_ref, gains_ref, idx_hbm, w_hbm, qa_hbm, ta_hbm, wk_hbm, wv_hbm, wo_hbm = refs[:9]
     arrays = refs[9:9 + n_arrays]
-    (joined_ref, normed_ref, top_ref, bottom_ref, edge_ref, table, res, mix,
+    (joined_ref, normed_ref, top_ref, bottom_ref, edge_ref, table, res,
      idx_ref, w_ref, qa_ref, ta_ref, wk_ref, wv_ref, wo_ref, stage, sems, stage_sems) = refs[9 + n_arrays:]
     copies = [
         pltpu.make_async_copy(src, dst, sems.at[n])
@@ -218,26 +217,22 @@
         following = jnp.minimum(t + 1, tiles - 1)
         units = [(l0, l1, q0) for l0, l1 in ((0, 256), (256, 384)) for q0 in range(0, rows, PART)]
         per = TILE // len(units)
+        parts = {}
         for n, (l0, l1, q0) in enumerate(units):
-            mixed = attend_heads(qa[q0:q0 + PART, l0:l1], kk[:, l0:l1], vv[:, l0:l1], None)
-            mix[pl.ds(pl.multiple_of(t * rows + q0, PART), PART), l0:l1] = mixed.astype(jnp.bfloat16)
+            parts[l0, q0] = attend_heads(qa[q0:q0 + PART, l0:l1], kk[:, l0:l1], vv[:, l0:l1], None).astype(jnp.bfloat16)
             for i in range(n * per, n * per + per):
                 line(following, i)
+        mix = jnp.concatenate(
+            [jnp.concatenate([parts[l0, q0] for l0 in (0, 256)], axis=1) for q0 in range(0, rows, PART)], axis=0)
+        o = jnp.dot(mix, wo_ref[...], preferred_element_type=jnp.float32)
+        cols = pl.ds(pl.multiple_of(t * TILE, TILE), TILE)
+        joined = (ta_ref[:, cols, :].reshape(rows, channels).astype(jnp.float32) + o).astype(jnp.bfloat16)
+        joined_ref[:, cols, :] = joined.reshape(TILE, TILE, channels)
+        normed_ref[:, cols, :] = rms_rows(joined.astype(jnp.float32), gains_ref[3:4, :]).astype(jnp.bfloat16).reshape(TILE, TILE, channels)
         return carry
 
     lax.fori_loop(0, tiles, attend, 0)
 
-    def finish(t, carry):
-        at = pl.ds(pl.multiple_of(t * (BATCH * rows), rows), BATCH * rows)
-        o = jnp.dot(mix[at, :], wo_ref[...], preferred_element_type=jnp.float32)
-        for n in range(BATCH):
-            cols = pl.ds(pl.multiple_of((t * BATCH + n) * TILE, TILE), TILE)
-            joined = (ta_ref[:, cols, :].reshape(rows, channels).astype(jnp.float32) + o[n * rows:(n + 1) * rows]).astype(jnp.bfloat16)
-            joined_ref[:, cols, :] = joined.reshape(TILE, TILE, channels)
-            normed_ref[:, cols, :] = rms_rows(joined.astype(jnp.float32), gains_ref[3:4, :]).astype(jnp.bfloat16).reshape(TILE, TILE, channels)
-        return carry
-
-    lax.fori_loop(0, tiles // BATCH, finish, 0)
     top_ref[...] = normed_ref[0:RIM]
     bottom_ref[...] = normed_ref[height - RIM:height]
     first_group = place_ref[1] == 0
@@ -269,15 +264,14 @@
         scratch_shapes=[
             pltpu.VMEM((n * piece_rows // 8, lanes, 8, 128), jnp.float32),
             pltpu.VMEM((total // 8, lanes, 8, 128), jnp.float32),
-            pltpu.VMEM((total, channels), jnp.bfloat16),
             pltpu.SMEM(idx.shape, jnp.int32),
             pltpu.SMEM(idx.shape, jnp.float32),
             pltpu.VMEM(ta.shape, jnp.bfloat16),
             pltpu.VMEM(ta.shape, jnp.bfloat16),
             square, square, square,
-            pltpu.VMEM((8, piece_rows, channels), jnp.bfloat16),
+            pltpu.VMEM((n, piece_rows, channels), jnp.bfloat16),
             pltpu.SemaphoreType.DMA((7,)),
-            pltpu.SemaphoreType.DMA((8,)),
+            pltpu.SemaphoreType.DMA((n,)),
         ],
         compiler_params=pltpu.CompilerParams(vmem_limit_bytes=60 << 20),
         cost_estimate=pl.CostEstimate(flops=30_000_000_000, transcendentals=0, bytes_accessed=10_000_000),

time: 145 us -> 144 us (level)
  no operation moved by 1% of the time
where the time goes in v2:
time: 144 us; the launch traced here: 143 us
  Pallas kernels  81.8 us (57%)
  starting transfers between devices  36.4 us (25%)
  waiting for transfers between devices  17.1 us (12%)
  local copies, waits for them, and re-layouts  7.31 us (5%)
    pallas_call x2, Pallas kernels, window_call(): pl.pallas_call(functools.partial(window_kernel, tuple(spans), tuple(plan)...  27.2 us
    pallas_call x1, Pallas kernels, gather_call(): pl.pallas_call(functools.partial(gather_kernel, tuple(plan), len(arrays),...  25.7 us
    ppermute x2, waiting for transfers between devices, near(): return lax.ppermute(rows, 'swath', pairs)  12.8 us
    pallas_call x1, Pallas kernels, first_call(): pl.pallas_call(functools.partial(first_kernel, STEP1), out_shape=jax.Shap...  9.03 us
    pallas_call x1, Pallas kernels, second_call(): pl.pallas_call(functools.partial(second_kernel, STEP2), out_shape=jax.Sha...  7.56 us
    pallas_call x1, Pallas kernels, rim_call(): pl.pallas_call(rim_kernel, out_shape=jax.ShapeDtypeStruct(joined.shape, j...  6.76 us
    ppermute x2, starting transfers between devices, far(): return lax.ppermute(rows, 'swath', relay)  6.61 us
    ppermute x6, starting transfers between devices, body(): swapped = lambda rows: lax.ppermute(rows, 'group', swap)  5.27 us
  transfers between devices with their start and end apart: 21, of which 5 were waited for; matrix products, arithmetic and copies ran while one was open for 2% of the time, Pallas kernels for 34%

profile of v2, /device:TPU:11, one launch (start us, length us, event | category | flops | bytes accessed | tf_op | source)
XLA Modules:
  0.0 143.4 jit_solution(4418520428027450320)
XLA Ops:
  0.0 0.9 constant_dynamic-slice_fusion.2
  0.9 0.7 collective-permute-start
  1.6 1.1 fusion
  2.8 3.0 %collective-permute-start.2 = (bf16[3,128,384]{2,1,0:T(8,128)(2,1)S(1)}, bf16[3,128,384]{2,1,0:T(8,128)(2,1)S(1)}, u32[]{:S(2)}, u32[]{:S(2)}) collective-permute-start(bf16[3,128,384]{2,1,0:T(8,128)(2,1)S(1)} %get-tuple-element.45), channel_id=1, source_target_pairs={{2,0},{4,2},{6,4},{8,6},{10,8},{12,10},{14,12},{3,1},{5,3},{7,5},{... | collective-permute-start | bytes 884744 | tf_op jit(solution)/shard_map/ppermute | solution.py:570
  5.8 2.2 %collective-permute-start.1 = (bf16[3,128,384]{2,1,0:T(8,128)(2,1)S(1)}, bf16[3,128,384]{2,1,0:T(8,128)(2,1)S(1)}, u32[]{:S(2)}, u32[]{:S(2)}) collective-permute-start(bf16[3,128,384]{2,1,0:T(8,128)(2,1)S(1)} %get-tuple-element.46), channel_id=1, source_target_pairs={{0,2},{2,4},{4,6},{6,8},{8,10},{10,12},{12,14},{1,3},{3,5},{5,7},{... | collective-permute-start | bytes 884744 | tf_op jit(solution)/shard_map/ppermute | solution.py:569
  8.1 0.7 stack.19.place_ref.refs_0_
  8.8 0.0 collective-permute-done.rest_1_.rest_5_.rest_6_
  8.8 0.6 copy-done.21
  9.4 13.1 %shard_map.190.refs_10_ = bf16[1024,384]{1,0:T(8,128)(2,1)} custom-call(s32[9]{0:T(128)} %stack.19.place_ref.refs_0_, f32[384]{0:T(512)} %gain_ref.3, bf16[384,384]{1,0:T(8,128)(2,1)} %wq_hbm.3, bf16[384,384]{1,0:T(8,128)(2,1)} %wk_hbm.3, bf16[384,384]{1,0:T(8,128)(2,1)} %wv_hbm.3, bf16[384,384]{1,0:T(8,128)(2,1)} %wo_hbm.3, bf16[16,128,384]{2,1,0:T(8,128)(2,1)} %rest_2_.1, ...), custom_call_target="tpu_custom_call" | custom-call | flops 14000000000 | bytes 4000000 | tf_op jit(solution)/shard_map/pallas_call | solution.py:123
  22.5 0.0 collective-permute-done.2.rest_3_
  22.6 0.0 collective-permute-done.1.rest_0_
  22.6 0.0 copy-start.11
  22.6 0.1 pad_maximum_fusion
  22.7 0.0 copy-start.15
  22.7 0.0 copy-start.16
  22.7 0.0 copy-start.17
  22.7 0.0 copy-start.18
  22.7 0.0 copy-start
  22.8 0.0 copy-start.2
  22.8 0.6 collective-permute-start.3
  23.4 2.2 %collective-permute-start.10 = (bf16[1024,384]{1,0:T(8,128)(2,1)}, bf16[1024,384]{1,0:T(8,128)(2,1)}, u32[]{:S(2)}, u32[]{:S(2)}) collective-permute-start(bf16[1024,384]{1,0:T(8,128)(2,1)} %shard_map.190.refs_10_), channel_id=1, source_target_pairs={{0,2},{2,0},{4,6},{6,4},{8,10},{10,8},{12,14},{14,12},{1,3},{3,1},... | collective-permute-start | bytes 2359304 | tf_op jit(solution)/shard_map/ppermute | solution.py:574
  25.6 0.0 collective-permute-done.3.rest_4_.rest_7_
  25.6 0.6 copy-done.22
  26.2 14.0 %shard_map.191.refs_9_ = bf16[1024,384]{1,0:T(8,128)(2,1)} custom-call(s32[9]{0:T(128)} %stack.19.place_ref.refs_0_, f32[384]{0:T(512)} %gain_ref.3, bf16[384,384]{1,0:T(8,128)(2,1)} %wq_hbm.3, bf16[384,384]{1,0:T(8,128)(2,1)} %wk_hbm.3, bf16[384,384]{1,0:T(8,128)(2,1)} %wv_hbm.3, bf16[384,384]{1,0:T(8,128)(2,1)} %wo_hbm.3, bf16[3,128,384]{2,1,0:T(8,128)(2,1)} %copy-done.11, ...), custom_call_target="tpu_custom_call" | custom-call | flops 14000000000 | bytes 4000000 | tf_op jit(solution)/shard_map/pallas_call | solution.py:123
  40.2 0.9 collective-permute-start.4
  41.2 0.7 collective-permute-start.9
  41.9 0.1 select_add_fusion.gains_ref.refs_1_
  41.9 1.8 %collective-permute-done.10.refs_14_ = bf16[1024,384]{1,0:T(8,128)(2,1)} collective-permute-done((bf16[1024,384]{1,0:T(8,128)(2,1)}, bf16[1024,384]{1,0:T(8,128)(2,1)}, u32[]{:S(2)}, u32[]{:S(2)}) %collective-permute-start.10) | collective-permute-done | bytes 786464 | tf_op jit(solution)/shard_map/ppermute | solution.py:574
  43.7 3.4 %collective-permute-start.14 = (bf16[1024,384]{1,0:T(8,128)(2,1)}, bf16[1024,384]{1,0:T(8,128)(2,1)}, u32[]{:S(2)}, u32[]{:S(2)}) collective-permute-start(bf16[1024,384]{1,0:T(8,128)(2,1)} %collective-permute-done.10.refs_14_), channel_id=1, source_target_pairs={{0,4},{4,8},{6,2},{8,12},{10,6},{14,10},{1,5},{5,9},{7,3},{9,13},{... | collective-permute-start | bytes 2359304 | tf_op jit(solution)/shard_map/ppermute | solution.py:577
  47.1 1.2 shard_map.194.refs_4_
  48.4 0.0 copy-start.1
  48.4 1.1 copy-done.1
  49.5 11.0 %collective-permute-done.4.refs_13_ = bf16[1024,384]{1,0:T(8,128)(2,1)} collective-permute-done((bf16[1024,384]{1,0:T(8,128)(2,1)}, bf16[1024,384]{1,0:T(8,128)(2,1)}, u32[]{:S(2)}, u32[]{:S(2)}) %collective-permute-start.4) | collective-permute-done | bytes 786464 | tf_op jit(solution)/shard_map/ppermute | solution.py:574
  60.6 3.2 %collective-permute-start.13 = (bf16[1024,384]{1,0:T(8,128)(2,1)}, bf16[1024,384]{1,0:T(8,128)(2,1)}, u32[]{:S(2)}, u32[]{:S(2)}) collective-permute-start(bf16[1024,384]{1,0:T(8,128)(2,1)} %collective-permute-done.4.refs_13_), channel_id=1, source_target_pairs={{0,4},{4,8},{6,2},{8,12},{10,6},{14,10},{1,5},{5,9},{7,3},{9,13},{... | collective-permute-start | bytes 2359304 | tf_op jit(solution)/shard_map/ppermute | solution.py:577
  63.8 1.5 %shard_map.192 = (s32[3,9,128]{2,1,0:T(8,128)}, s32[3,9,128]{2,1,0:T(8,128)}) custom-call(s32[9]{0:T(128)} %stack.19.place_ref.refs_0_, s32[16,1024]{1,0:T(8,128)} %bitcast.8, s32[1,16]{1,0:T(1,128)} %bitcast.11), custom_call_target="tpu_custom_call" | custom-call | flops 1000000 | bytes 100000 | tf_op jit(solution)/shard_map/pallas_call | solution.py:459
  65.3 0.9 collective-permute-start.5
  66.2 0.7 fusion.1
  66.9 0.3 collective-permute-done.5.taken_ref
  67.3 2.3 %collective-permute-start.6 = (s32[2,9,128]{2,1,0:T(8,128)S(1)}, s32[2,9,128]{2,1,0:T(8,128)S(1)}, u32[]{:S(2)}, u32[]{:S(2)}) collective-permute-start(s32[2,9,128]{2,1,0:T(8,128)S(1)} %pad_add_fusion), channel_id=1, source_target_pairs={{0,2},{2,4},{4,6},{6,8},{8,10},{10,12},{12,14},{1,3},{3,5},{5,7},{... | collective-permute-start | bytes 27656 | tf_op jit(solution)/shard_map/ppermute | solution.py:596
  69.6 3.9 %collective-permute-start.7 = (s32[2,9,128]{2,1,0:T(8,128)S(1)}, s32[2,9,128]{2,1,0:T(8,128)S(1)}, u32[]{:S(2)}, u32[]{:S(2)}) collective-permute-start(s32[2,9,128]{2,1,0:T(8,128)S(1)} %pad_add_fusion.1), channel_id=1, source_target_pairs={{2,0},{4,2},{6,4},{8,6},{10,8},{12,10},{14,12},{3,1},{5,3},{7,5},{... | collective-permute-start | bytes 27656 | tf_op jit(solution)/shard_map/ppermute | solution.py:597
  73.5 0.0 collective-permute-done.6.upper_ref
  73.5 1.0 collective-permute-start.8
  74.5 0.0 collective-permute-done.7.lower_ref
  74.5 1.3 collective-permute-start.12
  75.8 2.9 %shard_map.193 = (s32[64,128]{1,0:T(8,128)}, f32[64,128]{1,0:T(8,128)}) custom-call(s32[9]{0:T(128)} %stack.19.place_ref.refs_0_, s32[64,128]{1,0:T(8,128)} %bitcast.9, f32[64,128]{1,0:T(8,128)} %bitcast.10, s32[2,9,128]{2,1,0:T(8,128)} %copy-done.13, s32[3,9,128]{2,1,0:T(8,128)} %get-tuple-element.30.keep_ref, s32[3,9,128]{2,1,0:T(8,128)} %copy-done.12, ...), custom_call_target="tpu_custom_call" | custom-call | flops 1000000 | bytes 100000 | tf_op jit(solution)/shard_map/pallas_call | solution.py:493
  78.8 0.0 collective-permute-done.14.refs_18_
  78.8 0.7 collective-permute-start.11
  79.4 0.1 collective-permute-start.16
  79.5 1.7 %collective-permute-done.13.refs_17_ = bf16[1024,384]{1,0:T(8,128)(2,1)} collective-permute-done((bf16[1024,384]{1,0:T(8,128)(2,1)}, bf16[1024,384]{1,0:T(8,128)(2,1)}, u32[]{:S(2)}, u32[]{:S(2)}) %collective-permute-start.13) | collective-permute-done | bytes 786464 | tf_op jit(solution)/shard_map/ppermute | solution.py:577
  81.2 1.5 %collective-permute-start.15 = (bf16[1024,384]{1,0:T(8,128)(2,1)}, bf16[1024,384]{1,0:T(8,128)(2,1)}, u32[]{:S(2)}, u32[]{:S(2)}) collective-permute-start(bf16[1024,384]{1,0:T(8,128)(2,1)} %collective-permute-done.13.refs_17_), channel_id=1, source_target_pairs={{0,1},{1,0},{2,3},{3,2},{4,5},{5,4},{6,7},{7,6},{8,9},{9,8},{10,11... | collective-permute-start | bytes 2359304 | tf_op jit(solution)/shard_map/ppermute | solution.py:607
  82.7 0.0 collective-permute-done.8.refs_11_
  82.7 0.0 collective-permute-done.16.refs_20_
  82.7 2.2 %collective-permute-done.15.refs_19_ = bf16[1024,384]{1,0:T(8,128)(2,1)} collective-permute-done((bf16[1024,384]{1,0:T(8,128)(2,1)}, bf16[1024,384]{1,0:T(8,128)(2,1)}, u32[]{:S(2)}, u32[]{:S(2)}) %collective-permute-start.15) | collective-permute-done | bytes 786464 | tf_op jit(solution)/shard_map/ppermute | solution.py:607
  85.0 25.7 %shard_map.195 = (bf16[16,128,384]{2,1,0:T(8,128)(2,1)}, bf16[16,128,384]{2,1,0:T(8,128)(2,1)}, bf16[2,128,384]{2,1,0:T(8,128)(2,1)}, bf16[2,128,384]{2,1,0:T(8,128)(2,1)}, bf16[16,8,384]{2,1,0:T(8,128)(2,1)}) custom-call(s32[9]{0:T(128)} %stack.19.place_ref.refs_0_, f32[8,384]{1,0:T(8,128)} %copy-done.3, s32[64,128]{1,0:T(8,128)} %get-tuple-element.32.refs_2_, ...), custom_call_target="tpu_custom_call" | custom-call | flops 30000001024 | bytes 10000000 | tf_op jit(solution)/shard_map/pallas_call | solution.py:259
  110.6 0.4 collective-permute-start.17
  111.1 3.2 %collective-permute-start.18 = (bf16[2,128,384]{2,1,0:T(8,128)(2,1)}, bf16[2,128,384]{2,1,0:T(8,128)(2,1)S(1)}, u32[]{:S(2)}, u32[]{:S(2)}) collective-permute-start(bf16[2,128,384]{2,1,0:T(8,128)(2,1)} %get-tuple-element.41), channel_id=1, source_target_pairs={{0,2},{2,4},{4,6},{6,8},{8,10},{10,12},{12,14},{1,3},{3,5},{5,7},{... | collective-permute-start | bytes 589832 | tf_op jit(solution)/shard_map/ppermute | solution.py:620
  114.3 3.2 %collective-permute-start.19 = (bf16[2,128,384]{2,1,0:T(8,128)(2,1)}, bf16[2,128,384]{2,1,0:T(8,128)(2,1)S(1)}, u32[]{:S(2)}, u32[]{:S(2)}) collective-permute-start(bf16[2,128,384]{2,1,0:T(8,128)(2,1)} %get-tuple-element.42), channel_id=1, source_target_pairs={{2,0},{4,2},{6,4},{8,6},{10,8},{12,10},{14,12},{3,1},{5,3},{7,5},{... | collective-permute-start | bytes 589832 | tf_op jit(solution)/shard_map/ppermute | solution.py:621
  117.6 1.4 copy-done.8
  119.0 9.0 %shard_map.196.inner_ref = bf16[14,144,384]{2,1,0:T(8,128)(2,1)S(1)} custom-call(s32[9]{0:T(128)S(1)} %copy-done.4, bf16[16,128,384]{2,1,0:T(8,128)(2,1)S(1)} %copy-done.8, bf16[16,8,384]{2,1,0:T(8,128)(2,1)S(1)} %collective-permute-done.17.side_ref, bf16[3,3,384,384]{3,2,1,0:T(8,128)(2,1)S(1)} %copy-done.5), custom_call_target="tpu_custom_call" | custom-call | flops 10000000000 | bytes 4000000 | tf_op jit(solution)/shard_map/pallas_call | solution.py:393
  128.0 0.0 collective-permute-done.18.top_ref
  128.0 0.0 collective-permute-done.19.bottom_ref
  128.1 0.8 collective-permute-start.20
  128.9 7.6 %shard_map.197.merged_hbm = bf16[16,128,384]{2,1,0:T(8,128)(2,1)} custom-call(bf16[14,144,384]{2,1,0:T(8,128)(2,1)S(1)} %shard_map.196.inner_ref, bf16[16,128,384]{2,1,0:T(8,128)(2,1)S(1)} %copy-done.7, bf16[3,3,384,384]{3,2,1,0:T(8,128)(2,1)S(1)} %copy-done.6), custom_call_target="tpu_custom_call" | custom-call | flops 8000000000 | bytes 4000000 | tf_op jit(solution)/shard_map/pallas_call | solution.py:409
  136.5 6.8 %shard_map.198 = bf16[16,128,384]{2,1,0:T(8,128)(2,1)} custom-call(s32[9]{0:T(128)S(1)} %copy-done.4, bf16[16,128,384]{2,1,0:T(8,128)(2,1)S(1)} %copy-done.9, bf16[16,8,384]{2,1,0:T(8,128)(2,1)S(1)} %collective-permute-done.17.side_ref, bf16[2,128,384]{2,1,0:T(8,128)(2,1)S(1)} %collective-permute-done.18.top_ref, ...), custom_call_target="tpu_custom_call", output_to_operand_aliasing={{}: (10, {})} | custom-call | flops 5000000000 | bytes 4000000 | tf_op jit(solution)/shard_map/pallas_call | solution.py:422
  (47 shorter events, 0.2 us)
Async XLA Ops:
  0.9 7.9 %collective-permute-start = (bf16[16,8,384]{2,1,0:T(8,128)(2,1)S(1)}, bf16[16,8,384]{2,1,0:T(8,128)(2,1)S(1)}, u32[]{:S(2)}, u32[]{:S(2)}) collective-permute-start(bf16[16,8,384]{2,1,0:T(8,128)(2,1)S(1)} %constant_dynamic-slice_fusion.2), channel_id=1, source_target_pairs={{0,1},{1,0},{2,3},{3,2},{4,5},{5,4},{6,7},{7,6},{8,9},{9,8},{10,11... | collective-permute-start | bytes 294920 | tf_op jit(solution)/shard_map/ppermute | solution.py:568
  2.8 19.8 %collective-permute-start.2 = (bf16[3,128,384]{2,1,0:T(8,128)(2,1)S(1)}, bf16[3,128,384]{2,1,0:T(8,128)(2,1)S(1)}, u32[]{:S(2)}, u32[]{:S(2)}) collective-permute-start(bf16[3,128,384]{2,1,0:T(8,128)(2,1)S(1)} %get-tuple-element.45), channel_id=1, source_target_pairs={{2,0},{4,2},{6,4},{8,6},{10,8},{12,10},{14,12},{3,1},{5,3},{7,5},{... | collective-permute-start | bytes 884744 | tf_op jit(solution)/shard_map/ppermute | solution.py:570
  5.8 16.8 %collective-permute-start.1 = (bf16[3,128,384]{2,1,0:T(8,128)(2,1)S(1)}, bf16[3,128,384]{2,1,0:T(8,128)(2,1)S(1)}, u32[]{:S(2)}, u32[]{:S(2)}) collective-permute-start(bf16[3,128,384]{2,1,0:T(8,128)(2,1)S(1)} %get-tuple-element.46), channel_id=1, source_target_pairs={{0,2},{2,4},{4,6},{6,8},{8,10},{10,12},{12,14},{1,3},{3,5},{5,7},{... | collective-permute-start | bytes 884744 | tf_op jit(solution)/shard_map/ppermute | solution.py:569
  8.8 0.6 copy-start.21
  22.6 3.0 %copy-start.10 = (bf16[3,128,384]{2,1,0:T(8,128)(2,1)}, bf16[3,128,384]{2,1,0:T(8,128)(2,1)S(1)}, u32[]{:S(2)}) copy-start(bf16[3,128,384]{2,1,0:T(8,128)(2,1)S(1)} %collective-permute-done.2.rest_3_) | copy-start | bytes 884740
  22.6 3.0 %copy-start.11 = (bf16[3,128,384]{2,1,0:T(8,128)(2,1)}, bf16[3,128,384]{2,1,0:T(8,128)(2,1)S(1)}, u32[]{:S(2)}) copy-start(bf16[3,128,384]{2,1,0:T(8,128)(2,1)S(1)} %collective-permute-done.1.rest_0_) | copy-start | bytes 884740
  22.7 18.5 %copy-start.19 = (bf16[1024,384]{1,0:T(8,128)(2,1)S(1)}, bf16[1024,384]{1,0:T(8,128)(2,1)}, u32[]{:S(2)}) copy-start(bf16[1024,384]{1,0:T(8,128)(2,1)} %shard_map.190.refs_10_) | copy-start | bytes 2359300
  22.7 19.2 %copy-start.15 = (f32[384]{0:T(512)S(1)}, f32[384]{0:T(512)}, u32[]{:S(2)}) copy-start(f32[384]{0:T(512)} %param.37) | copy-start | bytes 4612
  22.7 19.1 %copy-start.16 = (f32[384]{0:T(512)S(1)}, f32[384]{0:T(512)}, u32[]{:S(2)}) copy-start(f32[384]{0:T(512)} %param.32) | copy-start | bytes 4612
  22.7 19.1 %copy-start.17 = (f32[384]{0:T(512)S(1)}, f32[384]{0:T(512)}, u32[]{:S(2)}) copy-start(f32[384]{0:T(512)} %param.31) | copy-start | bytes 4612
  22.7 19.1 %copy-start.18 = (f32[384]{0:T(512)S(1)}, f32[384]{0:T(512)}, u32[]{:S(2)}) copy-start(f32[384]{0:T(512)} %gain_ref.3) | copy-start | bytes 4612
  22.7 24.4 %copy-start = (bf16[16,128,384]{2,1,0:T(8,128)(2,1)S(1)}, bf16[16,128,384]{2,1,0:T(8,128)(2,1)}, u32[]{:S(2)}) copy-start(bf16[16,128,384]{2,1,0:T(8,128)(2,1)} %refs_5_) | copy-start | bytes 4718596
  22.8 24.4 %copy-start.2 = (bf16[384,384]{1,0:T(8,128)(2,1)S(1)}, bf16[384,384]{1,0:T(8,128)(2,1)}, u32[]{:S(2)}) copy-start(bf16[384,384]{1,0:T(8,128)(2,1)} %w_ref.1) | copy-start | bytes 884740
  22.8 2.8 %collective-permute-start.3 = (bf16[6,8,384]{2,1,0:T(8,128)(2,1)S(1)}, bf16[6,8,384]{2,1,0:T(8,128)(2,1)S(1)}, u32[]{:S(2)}, u32[]{:S(2)}) collective-permute-start(bf16[6,8,384]{2,1,0:T(8,128)(2,1)S(1)} %constant_dynamic-slice_fusion.1), channel_id=1, source_target_pairs={{0,1},{1,0},{2,3},{3,2},{4,5},{5,4},{6,7},{7,6},{8,9},{9,8},{10,11... | collective-permute-start | bytes 110600 | tf_op jit(solution)/shard_map/ppermute | solution.py:585
  23.4 20.3 %collective-permute-start.10 = (bf16[1024,384]{1,0:T(8,128)(2,1)}, bf16[1024,384]{1,0:T(8,128)(2,1)}, u32[]{:S(2)}, u32[]{:S(2)}) collective-permute-start(bf16[1024,384]{1,0:T(8,128)(2,1)} %shard_map.190.refs_10_), channel_id=1, source_target_pairs={{0,2},{2,0},{4,6},{6,4},{8,10},{10,8},{12,14},{14,12},{1,3},{3,1},... | collective-permute-start | bytes 2359304 | tf_op jit(solution)/shard_map/ppermute | solution.py:574
  25.6 0.6 copy-start.22
  40.2 20.3 %collective-permute-start.4 = (bf16[1024,384]{1,0:T(8,128)(2,1)}, bf16[1024,384]{1,0:T(8,128)(2,1)}, u32[]{:S(2)}, u32[]{:S(2)}) collective-permute-start(bf16[1024,384]{1,0:T(8,128)(2,1)} %shard_map.191.refs_9_), channel_id=1, source_target_pairs={{0,2},{2,0},{4,6},{6,4},{8,10},{10,8},{12,14},{14,12},{1,3},{3,1},... | collective-permute-start | bytes 2359304 | tf_op jit(solution)/shard_map/ppermute | solution.py:574
  41.2 38.3 %collective-permute-start.9 = (bf16[1024,384]{1,0:T(8,128)(2,1)S(1)}, bf16[1024,384]{1,0:T(8,128)(2,1)}, u32[]{:S(2)}, u32[]{:S(2)}) collective-permute-start(bf16[1024,384]{1,0:T(8,128)(2,1)S(1)} %copy-done.19), channel_id=1, source_target_pairs={{0,1},{1,0},{2,3},{3,2},{4,5},{5,4},{6,7},{7,6},{8,9},{9,8},{10,11... | collective-permute-start | bytes 2359304 | tf_op jit(solution)/shard_map/ppermute | solution.py:607
  41.9 6.4 %copy-start.3 = (f32[8,384]{1,0:T(8,128)}, f32[8,384]{1,0:T(8,128)S(1)}, u32[]{:S(2)}) copy-start(f32[8,384]{1,0:T(8,128)S(1)} %select_add_fusion.gains_ref.refs_1_) | copy-start | bytes 36868
  43.7 35.1 %collective-permute-start.14 = (bf16[1024,384]{1,0:T(8,128)(2,1)}, bf16[1024,384]{1,0:T(8,128)(2,1)}, u32[]{:S(2)}, u32[]{:S(2)}) collective-permute-start(bf16[1024,384]{1,0:T(8,128)(2,1)} %collective-permute-done.10.refs_14_), channel_id=1, source_target_pairs={{0,4},{4,8},{6,2},{8,12},{10,6},{14,10},{1,5},{5,9},{7,3},{9,13},{... | collective-permute-start | bytes 2359304 | tf_op jit(solution)/shard_map/ppermute | solution.py:577
  48.4 1.1 copy-start.1
  60.6 20.6 %collective-permute-start.13 = (bf16[1024,384]{1,0:T(8,128)(2,1)}, bf16[1024,384]{1,0:T(8,128)(2,1)}, u32[]{:S(2)}, u32[]{:S(2)}) collective-permute-start(bf16[1024,384]{1,0:T(8,128)(2,1)} %collective-permute-done.4.refs_13_), channel_id=1, source_target_pairs={{0,4},{4,8},{6,2},{8,12},{10,6},{14,10},{1,5},{5,9},{7,3},{9,13},{... | collective-permute-start | bytes 2359304 | tf_op jit(solution)/shard_map/ppermute | solution.py:577
  65.3 2.0 %collective-permute-start.5 = (s32[3,9,128]{2,1,0:T(8,128)}, s32[3,9,128]{2,1,0:T(8,128)S(1)}, u32[]{:S(2)}, u32[]{:S(2)}) collective-permute-start(s32[3,9,128]{2,1,0:T(8,128)} %get-tuple-element.31), channel_id=1, source_target_pairs={{0,1},{1,0},{2,3},{3,2},{4,5},{5,4},{6,7},{7,6},{8,9},{9,8},{10,11... | collective-permute-start | bytes 41480 | tf_op jit(solution)/shard_map/ppermute | solution.py:595
  67.3 8.6 %copy-start.12 = (s32[3,9,128]{2,1,0:T(8,128)}, s32[3,9,128]{2,1,0:T(8,128)S(1)}, u32[]{:S(2)}) copy-start(s32[3,9,128]{2,1,0:T(8,128)S(1)} %collective-permute-done.5.taken_ref) | copy-start | bytes 41476
  67.3 6.2 %collective-permute-start.6 = (s32[2,9,128]{2,1,0:T(8,128)S(1)}, s32[2,9,128]{2,1,0:T(8,128)S(1)}, u32[]{:S(2)}, u32[]{:S(2)}) collective-permute-start(s32[2,9,128]{2,1,0:T(8,128)S(1)} %pad_add_fusion), channel_id=1, source_target_pairs={{0,2},{2,4},{4,6},{6,8},{8,10},{10,12},{12,14},{1,3},{3,5},{5,7},{... | collective-permute-start | bytes 27656 | tf_op jit(solution)/shard_map/ppermute | solution.py:596
  69.6 4.9 %collective-permute-start.7 = (s32[2,9,128]{2,1,0:T(8,128)S(1)}, s32[2,9,128]{2,1,0:T(8,128)S(1)}, u32[]{:S(2)}, u32[]{:S(2)}) collective-permute-start(s32[2,9,128]{2,1,0:T(8,128)S(1)} %pad_add_fusion.1), channel_id=1, source_target_pairs={{2,0},{4,2},{6,4},{8,6},{10,8},{12,10},{14,12},{3,1},{5,3},{7,5},{... | collective-permute-start | bytes 27656 | tf_op jit(solution)/shard_map/ppermute | solution.py:597
  73.5 2.3 %copy-start.13 = (s32[2,9,128]{2,1,0:T(8,128)}, s32[2,9,128]{2,1,0:T(8,128)S(1)}, u32[]{:S(2)}) copy-start(s32[2,9,128]{2,1,0:T(8,128)S(1)} %collective-permute-done.6.upper_ref) | copy-start | bytes 27652
  73.5 9.2 %collective-permute-start.8 = (bf16[1024,384]{1,0:T(8,128)(2,1)}, bf16[1024,384]{1,0:T(8,128)(2,1)}, u32[]{:S(2)}, u32[]{:S(2)}) collective-permute-start(bf16[1024,384]{1,0:T(8,128)(2,1)} %shard_map.191.refs_9_), channel_id=1, source_target_pairs={{0,1},{1,0},{2,3},{3,2},{4,5},{5,4},{6,7},{7,6},{8,9},{9,8},{10,11... | collective-permute-start | bytes 2359304 | tf_op jit(solution)/shard_map/ppermute | solution.py:607
  74.5 1.3 copy-start.14
  74.5 8.2 %collective-permute-start.12 = (bf16[1024,384]{1,0:T(8,128)(2,1)}, bf16[1024,384]{1,0:T(8,128)(2,1)}, u32[]{:S(2)}, u32[]{:S(2)}) collective-permute-start(bf16[1024,384]{1,0:T(8,128)(2,1)} %collective-permute-done.10.refs_14_), channel_id=1, source_target_pairs={{0,1},{1,0},{2,3},{3,2},{4,5},{5,4},{6,7},{7,6},{8,9},{9,8},{10,11... | collective-permute-start | bytes 2359304 | tf_op jit(solution)/shard_map/ppermute | solution.py:607
  78.7 38.8 %copy-start.4 = (s32[9]{0:T(128)S(1)}, s32[9]{0:T(128)}, u32[]{:S(2)}) copy-start(s32[9]{0:T(128)} %stack.19.place_ref.refs_0_) | copy-start | bytes 112
  78.7 38.8 %copy-start.5 = (bf16[3,3,384,384]{3,2,1,0:T(8,128)(2,1)S(1)}, bf16[3,3,384,384]{3,2,1,0:T(8,128)(2,1)}, u32[]{:S(2)}) copy-start(bf16[3,3,384,384]{3,2,1,0:T(8,128)(2,1)} %w1_hbm.1) | copy-start | bytes 7962628
  78.8 4.0 %collective-permute-start.11 = (bf16[1024,384]{1,0:T(8,128)(2,1)}, bf16[1024,384]{1,0:T(8,128)(2,1)}, u32[]{:S(2)}, u32[]{:S(2)}) collective-permute-start(bf16[1024,384]{1,0:T(8,128)(2,1)} %collective-permute-done.4.refs_13_), channel_id=1, source_target_pairs={{0,1},{1,0},{2,3},{3,2},{4,5},{5,4},{6,7},{7,6},{8,9},{9,8},{10,11... | collective-permute-start | bytes 2359304 | tf_op jit(solution)/shard_map/ppermute | solution.py:607
  79.4 3.3 %collective-permute-start.16 = (bf16[1024,384]{1,0:T(8,128)(2,1)}, bf16[1024,384]{1,0:T(8,128)(2,1)S(1)}, u32[]{:S(2)}, u32[]{:S(2)}) collective-permute-start(bf16[1024,384]{1,0:T(8,128)(2,1)} %collective-permute-done.14.refs_18_), channel_id=1, source_target_pairs={{0,1},{1,0},{2,3},{3,2},{4,5},{5,4},{6,7},{7,6},{8,9},{9,8},{10,11... | collective-permute-start | bytes 2359304 | tf_op jit(solution)/shard_map/ppermute | solution.py:607
  81.2 3.8 %collective-permute-start.15 = (bf16[1024,384]{1,0:T(8,128)(2,1)}, bf16[1024,384]{1,0:T(8,128)(2,1)}, u32[]{:S(2)}, u32[]{:S(2)}) collective-permute-start(bf16[1024,384]{1,0:T(8,128)(2,1)} %collective-permute-done.13.refs_17_), channel_id=1, source_target_pairs={{0,1},{1,0},{2,3},{3,2},{4,5},{5,4},{6,7},{7,6},{8,9},{9,8},{10,11... | collective-permute-start | bytes 2359304 | tf_op jit(solution)/shard_map/ppermute | solution.py:607
  82.7 2.2 %copy-start.20 = (bf16[1024,384]{1,0:T(8,128)(2,1)}, bf16[1024,384]{1,0:T(8,128)(2,1)S(1)}, u32[]{:S(2)}) copy-start(bf16[1024,384]{1,0:T(8,128)(2,1)S(1)} %collective-permute-done.16.refs_20_) | copy-start | bytes 2359300
  110.6 6.9 %collective-permute-start.17 = (bf16[16,8,384]{2,1,0:T(8,128)(2,1)}, bf16[16,8,384]{2,1,0:T(8,128)(2,1)S(1)}, u32[]{:S(2)}, u32[]{:S(2)}) collective-permute-start(bf16[16,8,384]{2,1,0:T(8,128)(2,1)} %get-tuple-element.40), channel_id=1, source_target_pairs={{0,1},{1,0},{2,3},{3,2},{4,5},{5,4},{6,7},{7,6},{8,9},{9,8},{10,11... | collective-permute-start | bytes 294920 | tf_op jit(solution)/shard_map/ppermute | solution.py:619
  111.1 16.9 %collective-permute-start.18 = (bf16[2,128,384]{2,1,0:T(8,128)(2,1)}, bf16[2,128,384]{2,1,0:T(8,128)(2,1)S(1)}, u32[]{:S(2)}, u32[]{:S(2)}) collective-permute-start(bf16[2,128,384]{2,1,0:T(8,128)(2,1)} %get-tuple-element.41), channel_id=1, source_target_pairs={{0,2},{2,4},{4,6},{6,8},{8,10},{10,12},{12,14},{1,3},{3,5},{5,7},{... | collective-permute-start | bytes 589832 | tf_op jit(solution)/shard_map/ppermute | solution.py:620
  114.3 13.7 %collective-permute-start.19 = (bf16[2,128,384]{2,1,0:T(8,128)(2,1)}, bf16[2,128,384]{2,1,0:T(8,128)(2,1)S(1)}, u32[]{:S(2)}, u32[]{:S(2)}) collective-permute-start(bf16[2,128,384]{2,1,0:T(8,128)(2,1)} %get-tuple-element.42), channel_id=1, source_target_pairs={{2,0},{4,2},{6,4},{8,6},{10,8},{12,10},{14,12},{3,1},{5,3},{7,5},{... | collective-permute-start | bytes 589832 | tf_op jit(solution)/shard_map/ppermute | solution.py:621
  117.6 1.4 copy-start.8
  119.0 9.9 %copy-start.6 = (bf16[3,3,384,384]{3,2,1,0:T(8,128)(2,1)S(1)}, bf16[3,3,384,384]{3,2,1,0:T(8,128)(2,1)}, u32[]{:S(2)}) copy-start(bf16[3,3,384,384]{3,2,1,0:T(8,128)(2,1)} %w2_hbm.1) | copy-start | bytes 7962628
  119.0 9.9 %copy-start.7 = (bf16[16,128,384]{2,1,0:T(8,128)(2,1)S(1)}, bf16[16,128,384]{2,1,0:T(8,128)(2,1)}, u32[]{:S(2)}) copy-start(bf16[16,128,384]{2,1,0:T(8,128)(2,1)} %get-tuple-element.44.joined_ref) | copy-start | bytes 4718596
  128.1 8.4 %collective-permute-start.20 = (bf16[4,8,384]{2,1,0:T(8,128)(2,1)S(1)}, bf16[4,8,384]{2,1,0:T(8,128)(2,1)S(1)}, u32[]{:S(2)}, u32[]{:S(2)}) collective-permute-start(bf16[4,8,384]{2,1,0:T(8,128)(2,1)S(1)} %constant_dynamic-slice_fusion), channel_id=1, source_target_pairs={{0,1},{1,0},{2,3},{3,2},{4,5},{5,4},{6,7},{7,6},{8,9},{9,8},{10,11... | collective-permute-start | bytes 73736 | tf_op jit(solution)/shard_map/ppermute | solution.py:624
  128.9 7.6 %copy-start.9 = (bf16[16,128,384]{2,1,0:T(8,128)(2,1)S(1)}, bf16[16,128,384]{2,1,0:T(8,128)(2,1)}, u32[]{:S(2)}) copy-start(bf16[16,128,384]{2,1,0:T(8,128)(2,1)} %get-tuple-element.39.nc_ref) | copy-start | bytes 4718596
